TPU v7x, 128 devices: a whole 4x4x4 slice. The times are simulated.
128 devices in a mesh: grp: 32 (over z, y, core), tp: 4 (over x).
Axes of the slice: x: 4, y: 4, z: 4, core: 2. Of those that a mesh axis runs over, the one named last changes fastest.
Arguments:
- tokens: bfloat16 [32768, 2048], P('grp', 'tp'), may hold values from -6 to 6
- ln_gain: float32 [2048], replicated, may hold values from 0.25 to 1.75
- ln_bias: float32 [2048], replicated, may hold values from -3 to 3
- w_qkv: bfloat16 [2048, 6144], P(None, 'tp'), may hold values from -0.5 to 0.5
- b_qkv: float32 [6144], P('tp'), may hold values from -3 to 3
- w_out: bfloat16 [2048, 2048], P('tp'), may hold values from -0.125 to 0.125
- b_out: float32 [2048], P('tp'), may hold values from -3 to 3
- kv_cache: bfloat16 [65536, 4096], P('grp', 'tp'), may hold values from -24 to 24
- prefix_len: int32 [32], replicated, may hold values from 1 to 2048, as said below
- kv_pages: bfloat16 [256, 3, 128, 4096], P('grp', None, None, 'tp'), may hold values from -6 to 6
- page_table: int32 [256, 2], P('grp'), may hold values from 0 to 15, as said below
Outputs:
- mixed: bfloat16 [32768, 2048], P('grp', 'tp')
- decode_pages: bfloat16 [32, 16, 3, 128, 2048], P('grp', None, None, None, 'tp')
Inputs may be any that keep to these rules, and one draw needn't show every extreme that they name: prefix_len: every group between 1 and 2048, and some group exactly 2048. page_table: column 0 a request below 16, column 1 a slot below 16; every (request, slot) pair is named by exactly one page row; the 8 rows of one group name each request once or not at all.
All inputs are finite; a program needn't handle non-finite values.
Results may differ from a plain program's by a relative error of at most 0.027.
Values may be sent and summed in bfloat16 or wider, within the bound.
A program may use at most 192 MiB of HBM per device.

v0:
```python
import jax
import jax.numpy as jnp
from jax import lax
from jax.sharding import PartitionSpec as P

HEADS = 16
BLK = 512


NEG = -1e30
EPS = 1e-05


def block_update(carried, queries, key_block, value_block, allowed):
    highest, totals, running = carried
    scores = jnp.einsum("chd,khd->hck", queries, key_block, preferred_element_type=jnp.float32)
    scores = jnp.where(allowed, scores, NEG)
    raised = jnp.maximum(highest, jnp.max(scores, axis=2))
    factor = jnp.exp(highest - raised)
    expo = jnp.exp(scores - raised[:, :, None])
    totals = totals * factor + jnp.sum(expo, axis=2)
    running = running * factor[:, :, None] + jnp.einsum(
        "hck,khd->hcd", expo.astype(jnp.bfloat16), value_block, preferred_element_type=jnp.float32
    )
    return (raised, totals, running)


def cache_pass(carried, queries, stored, length, first_block, last_block, base_row):

    def visit(number, state):
        offset = number * BLK
        block_rows = lax.dynamic_slice_in_dim(stored, offset - base_row, BLK, 0)
        allowed = offset + jnp.arange(BLK) < length
        return block_update(
            state, queries, block_rows[:, :, 0, :], block_rows[:, :, 1, :], allowed[None, None, :]
        )

    return lax.fori_loop(first_block, last_block, visit, carried)


def move_pages(kv_pages, page_table):
    group_count = lax.axis_size("grp")
    page_count, layers, page_len, full_width = kv_pages.shape
    half_width = full_width // 2
    per_peer = max(1, page_count // (group_count // 2))
    slot_count = 2 * page_count
    wanted = page_table[:, 0]
    slot_ids = page_table[:, 1]
    order = jnp.arange(page_count)
    earlier = jnp.sum(
        (wanted[None, :] == wanted[:, None]) & (order[None, :] < order[:, None]), axis=1
    )
    halves = kv_pages.reshape(page_count, layers, page_len, 2, half_width)
    outgoing = jnp.zeros((group_count * per_peer, layers, page_len, half_width), jnp.bfloat16)
    labels = jnp.full((group_count * per_peer,), slot_count, jnp.int32)
    for parity in range(2):
        target = (2 * wanted + parity) * per_peer + earlier
        outgoing = outgoing.at[target].set(halves[:, :, :, parity, :])
        labels = labels.at[target].set(slot_ids)
    arrived, arrived_labels = (
        lax.all_to_all(outgoing, "grp", split_axis=0, concat_axis=0, tiled=True),
        lax.all_to_all(labels, "grp", split_axis=0, concat_axis=0, tiled=True),
    )
    placed = jnp.zeros((slot_count, layers, page_len, half_width), jnp.bfloat16)
    placed = placed.at[arrived_labels].set(arrived, mode="drop")
    return placed[None]


def shards(
    tokens, ln_gain, ln_bias, w_qkv, b_qkv, w_out, b_out, kv_cache, prefix_len, kv_pages, page_table
):
    tp_count = lax.axis_size("tp")
    span_rows, local_width = tokens.shape
    wide = tokens.astype(jnp.float32)
    whole = lax.all_gather(tokens, "tp", axis=1, tiled=True).astype(jnp.float32)
    center = jnp.mean(whole, axis=1, keepdims=True)
    spread = jnp.mean(whole * whole, axis=1, keepdims=True) - center * center
    normed = ((whole - center) * lax.rsqrt(spread + EPS) * ln_gain + ln_bias).astype(jnp.bfloat16)
    head_count = HEADS // tp_count
    head_size = w_qkv.shape[1] // (3 * head_count)
    projected = jnp.dot(normed, w_qkv, preferred_element_type=jnp.float32) + b_qkv
    projected = projected.reshape(span_rows, 3, head_count, head_size)
    queries = (projected[:, 0] * head_size ** (-0.5)).astype(jnp.bfloat16)
    new_keys = projected[:, 1].astype(jnp.bfloat16)
    new_values = projected[:, 2].astype(jnp.bfloat16)
    starting = (
        jnp.full((head_count, span_rows), NEG, jnp.float32),
        jnp.zeros((head_count, span_rows), jnp.float32),
        jnp.zeros((head_count, span_rows, head_size), jnp.float32),
    )
    query_row = jnp.arange(span_rows)
    causal = (query_row[None, :] <= query_row[:, None])[None]
    carried = block_update(starting, queries, new_keys, new_values, causal)
    prefix_rows = kv_cache.shape[0]
    stored = kv_cache.reshape(prefix_rows, head_count, 2, head_size)
    group_index = lax.axis_index("grp")
    own_length = prefix_len[group_index]
    own_blocks = (own_length + BLK - 1) // BLK
    carried = cache_pass(carried, queries, stored, own_length, 0, own_blocks, 0)
    attended = (carried[2] / carried[1][:, :, None]).astype(jnp.bfloat16)
    terms = jnp.einsum(
        "hcd,hde->ce",
        attended,
        w_out.reshape(head_count, head_size, w_out.shape[1]),
        preferred_element_type=jnp.float32,
    )
    summed = lax.psum_scatter(
        terms.astype(jnp.bfloat16), "tp", scatter_dimension=1, tiled=True
    ).astype(jnp.float32)
    mixed = (wide + summed + b_out).astype(jnp.bfloat16)
    decode_pages = move_pages(kv_pages, page_table)
    return (mixed, decode_pages)


def solution(mesh):
    placed = (
        P("grp", "tp"),
        P(),
        P(),
        P(None, "tp"),
        P("tp"),
        P("tp", None),
        P("tp"),
        P("grp", "tp"),
        P(),
        P("grp", None, None, "tp"),
        P("grp", None),
    )
    return jax.shard_map(
        shards,
        mesh=mesh,
        in_specs=placed,
        out_specs=(P("grp", "tp"), P("grp", None, None, None, "tp")),
        check_vma=False,
    )
```

profile of v0, /device:TPU:0, one launch (start us, length us, event | category | flops | bytes accessed | tf_op | source)
XLA Modules:
  0.0 350.8 jit_solution(5454506367585378376)
XLA Ops:
  7.2 0.0 copy-start
  7.2 0.0 all-gather.2.cloned.1.call-start
  7.2 0.7 all-gather.2.cloned.1.call-update
  7.9 0.7 slice_bitcast_fusion.7
  8.6 0.2 convert_reduce_fusion.1
  8.8 0.8 fusion.40
  9.5 0.6 scatter_custom_fusion
  10.1 0.6 scatter_fusion
  10.8 0.7 copy.59
  11.4 8.4 %all-to-all-start = ((s32[32,1,1]{2,1,0:T(1,128)}), s32[32,1,1]{2,1,0:T(1,128)S(1)}, u32[]{:S(2)}, u32[]{:S(2)}) async-start(s32[32,1,1]{2,1,0:T(1,128)} %copy.59), calls=%async_computation.1 | async-start | bytes 32768 | tf_op jit(solution)/shard_map/all_to_all | solution.py:62
  19.9 1.3 dynamic_slice.6
  21.9 6.6 %copy.57 = bf16[2048,1024]{0,1:T(8,128)(2,1)} copy(bf16[2048,1024]{1,0:T(8,128)(2,1)} %param.20) | data formatting | bytes 8388608 | tf_op args[7]
  28.5 8.6 %copy.60 = bf16[8,3,128,1024]{2,3,1,0:T(8,128)(2,1)} copy(bf16[8,3,128,1024]{3,2,1,0:T(8,128)(2,1)} %param.22) | data formatting | bytes 12582912 | tf_op args[9]
  37.1 6.3 %slice_bitcast_fusion = (bf16[8,3,128,512]{2,3,1,0:T(8,128)(2,1)}, bf16[8,3,128,512]{2,3,1,0:T(8,128)(2,1)}) fusion(bf16[8,3,128,2,512]{2,4,3,1,0:T(8,128)(2,1)} %bitcast.82), kind=kLoop, calls=%fused_computation.47 | loop fusion | bytes 12582912 | tf_op jit(solution)/shard_map/squeeze | solution.py:58
  43.4 4.6 %copy.61 = bf16[8,3,128,512]{3,2,1,0:T(8,128)(2,1)} copy(bf16[8,3,128,512]{2,3,1,0:T(8,128)(2,1)} %get-tuple-element.111) | data formatting | bytes 6291456 | tf_op jit(solution)/shard_map/squeeze | solution.py:58
  48.0 4.7 %copy.62 = bf16[8,3,128,512]{3,2,1,0:T(8,128)(2,1)} copy(bf16[8,3,128,512]{2,3,1,0:T(8,128)(2,1)} %get-tuple-element.110) | data formatting | bytes 6291456 | tf_op jit(solution)/shard_map/squeeze | solution.py:58
  52.7 6.1 %broadcast_in_dim.42 = bf16[32,3,128,512]{3,2,1,0:T(8,128)(2,1)} broadcast(bf16[]{:T(256)} %constant.67.clone.1), dimensions={} | broadcast | bytes 12582914 | tf_op jit(solution)/shard_map/broadcast_in_dim | solution.py:54
  58.8 9.8 %scatter_fusion.1 = bf16[32,3,128,512]{3,2,1,0:T(8,128)(2,1)} fusion(bf16[32,3,128,512]{3,2,1,0:T(8,128)(2,1)} %broadcast_in_dim.42, s32[8]{0:T(128)S(1)} %get-tuple-element.117, bf16[8,3,128,512]{3,2,1,0:T(8,128)(2,1)} %copy.61), kind=kCustom, calls=%fused_computation.2 | custom fusion | bytes 9437216 | tf_op jit(solution)/shard_map/scatter | solution.py:58
  68.7 9.9 %scatter_fusion.2 = bf16[32,3,128,512]{3,2,1,0:T(8,128)(2,1)} fusion(bf16[32,3,128,512]{3,2,1,0:T(8,128)(2,1)} %scatter_fusion.1, s32[8]{0:T(128)S(1)} %get-tuple-element.116, bf16[8,3,128,512]{3,2,1,0:T(8,128)(2,1)} %copy.62), kind=kCustom, calls=%fused_computation.3 | custom fusion | bytes 9437216 | tf_op jit(solution)/shard_map/scatter | solution.py:58
  78.5 1.3 iota_compare_fusion
  79.8 3.4 convert_reduce_fusion
  83.3 0.0 copy-done.7
  83.3 0.0 copy-done.8
  83.3 0.0 copy-done.9
  83.3 12.3 %convolution_add_fusion = f32[1024,1536]{1,0:T(8,128)} fusion(bf16[2048,1536]{1,0:T(8,128)(2,1)} %param.16, bf16[1024,2048]{1,0:T(8,128)(2,1)} %all-gather.2.cloned.1.call-done, f32[2048]{0:T(1024)S(1)} %copy-done.7, f32[2048]{0:T(1024)S(1)} %copy-done.8, f32[1024]{0:T(1024)S(1)} %get-tuple-element.115, f32[1024]{0:T(1024)S(1)} %get-tuple-element.114, ...), kind=kOutput, calls=%fused_computation.41 | convolution fusion | flops 6456606720 | bytes 16807936 | tf_op jit(solution)/shard_map/dot_general | solution.py:81
  95.6 7.7 %reshape.103 = f32[1024,3,4,128]{3,2,1,0:T(4,128)} reshape(f32[1024,1536]{1,0:T(8,128)} %convolution_add_fusion) | data formatting | bytes 12582912 | tf_op jit(solution)/shard_map/reshape | solution.py:82
  103.3 3.5 copy.54
  106.7 1.1 copy-done.2
  107.9 0.7 copy.69
  108.5 0.0 copy-start.4
  108.6 0.2 fusion.35
  108.8 0.3 copy-done.3
  109.1 7.1 %select_reduce_fusion = (f32[4,1024]{1,0:T(4,128)S(1)}, f32[4,1024,1024]{1,2,0:T(8,128)}) fusion(pred[1024,1024]{0,1:T(8,128)(4,1)S(1)} %copy-done.3, bf16[1024,4,128]{2,0,1:T(8,128)(2,1)S(1)} %fusion.35, bf16[1024,3,4,128]{3,0,2,1:T(8,128)(2,1)S(1)} %copy.69), kind=kOutput, calls=%fused_computation.25 | convolution fusion | flops 1082126336 | bytes 19939328 | tf_op jit(solution)/shard_map/chd,khd->hck/dot_general | solution.py:16
  116.2 9.0 %fusion.15 = f32[4,1024]{1,0:T(4,128)S(1)} fusion(f32[4,1024,1024]{1,2,0:T(8,128)} %get-tuple-element.120, f32[4,1024]{1,0:T(4,128)S(1)} %broadcast_maximum_fusion, pred[1024,1024]{0,1:T(8,128)(4,1)} %iota_compare_fusion), kind=kLoop, calls=%fused_computation.27 | loop fusion | flops 12578816 | bytes 17858560 | tf_op jit(solution)/shard_map/reduce_sum | solution.py:21
  125.3 9.8 %fusion.32 = f32[4,1024,128]{2,1,0:T(8,128)} fusion(f32[4,1024,1024]{1,2,0:T(8,128)} %get-tuple-element.120, f32[4,1024]{1,0:T(4,128)S(1)} %broadcast_maximum_fusion, pred[1024,1024]{0,1:T(8,128)(4,1)} %iota_compare_fusion, bf16[1024,3,4,128]{3,0,2,1:T(8,128)(2,1)} %copy-done.4, f32[4,1024]{1,0:T(4,128)S(1)} %get-tuple-element.112), kind=kOutput, calls=%fused_computation.53 | convolution fusion | flops 1086849024 | bytes 21004288 | tf_op jit(solution)/shard_map/hck,khd->hcd/dot_general | solution.py:22
  135.0 0.0 all-to-all-done
  135.0 7.4 %all-to-all-start.1 = ((bf16[32,3,128,512]{3,2,1,0:T(8,128)(2,1)}), bf16[32,3,128,512]{3,2,1,0:T(8,128)(2,1)}, u32[]{:S(2)}, u32[]{:S(2)}) async-start(bf16[32,3,128,512]{3,2,1,0:T(8,128)(2,1)} %scatter_fusion.2), calls=%async_computation.2 | async-start | bytes 25165824 | tf_op jit(solution)/shard_map/all_to_all | solution.py:61
  142.5 0.0 reduce-scatter.2.cloned.1.call-start
  142.5 49.0 %while.14 = (s32[]{:T(128)}, f32[4,1024]{1,0:T(4,128)S(1)}, f32[4,1024]{1,0:T(4,128)S(1)}, f32[4,1024,128]{2,1,0:T(8,128)}, s32[]{:T(128)}, /*index=5*/s32[]{:T(...) while((s32[]{:T(128)}, f32[4,1024]{1,0:T(4,128)S(1)}, ...), condition=%wide.region_7.8_spmd, body=%wide.region_4.7_spmd.sunk | while | flops 1091576832 | bytes 65276132 | solution.py:38
  142.5 0.6 add_compare_fusion.2
  143.2 2.7 bitcast_reduce_fusion.2
  146.0 3.3 copy-done.1
  149.3 1.7 fusion.55
  151.0 7.9 %multiply_add_fusion.5 = f32[4,1024,128]{2,1,0:T(8,128)} fusion(f32[4,1024,128]{2,1,0:T(8,128)} %get-tuple-element.195, f32[4,512,1024]{2,1,0:T(8,128)} %copy-done.1, f32[4,1024]{1,0:T(4,128)S(1)} %max.4, pred[512]{0:T(512)(128)(4,1)S(1)} %add_compare_fusion.2, f32[4,1024]{1,0:T(4,128)S(1)} %get-tuple-element.178, ...), kind=kOutput, calls=%fused_computation.14.clone.1 | convolution fusion | flops 544210944 | bytes 13140488 | tf_op jit(solution)/shard_map/while/body/hck,khd->hcd/dot_general | solution.py:22
  158.9 0.6 add_compare_fusion.2
  159.5 2.7 bitcast_reduce_fusion.2
  162.3 3.3 copy-done.1
  165.6 1.7 fusion.55
  167.3 7.9 %multiply_add_fusion.5 = f32[4,1024,128]{2,1,0:T(8,128)} fusion(f32[4,1024,128]{2,1,0:T(8,128)} %get-tuple-element.195, f32[4,512,1024]{2,1,0:T(8,128)} %copy-done.1, f32[4,1024]{1,0:T(4,128)S(1)} %max.4, pred[512]{0:T(512)(128)(4,1)S(1)} %add_compare_fusion.2, f32[4,1024]{1,0:T(4,128)S(1)} %get-tuple-element.178, ...), kind=kOutput, calls=%fused_computation.14.clone.1 | convolution fusion | flops 544210944 | bytes 13140488 | tf_op jit(solution)/shard_map/while/body/hck,khd->hcd/dot_general | solution.py:22
  175.2 0.6 add_compare_fusion.2
  175.9 2.7 bitcast_reduce_fusion.2
  178.6 0.0 copy-start.1
  178.6 3.3 copy-done.1
  181.9 1.7 fusion.55
  183.7 7.9 %multiply_add_fusion.5 = f32[4,1024,128]{2,1,0:T(8,128)} fusion(f32[4,1024,128]{2,1,0:T(8,128)} %get-tuple-element.195, f32[4,512,1024]{2,1,0:T(8,128)} %copy-done.1, f32[4,1024]{1,0:T(4,128)S(1)} %max.4, pred[512]{0:T(512)(128)(4,1)S(1)} %add_compare_fusion.2, f32[4,1024]{1,0:T(4,128)S(1)} %get-tuple-element.178, ...), kind=kOutput, calls=%fused_computation.14.clone.1 | convolution fusion | flops 544210944 | bytes 13140488 | tf_op jit(solution)/shard_map/while/body/hck,khd->hcd/dot_general | solution.py:22
  191.5 0.0 copy-done
  191.6 5.8 %bitcast_convert_fusion = bf16[1024,2048]{1,0:T(8,128)(2,1)} fusion(bf16[4,128,2048]{2,1,0:T(8,128)(2,1)S(1)} %bitcast.79, f32[4,1024,128]{2,1,0:T(8,128)} %get-tuple-element.46, f32[4,1024]{1,0:T(4,128)S(1)} %get-tuple-element.47), kind=kOutput, calls=%fused_computation.37 | convolution fusion | flops 2150629376 | bytes 8404992 | tf_op jit(solution)/shard_map/hcd,hde->ce/dot_general | solution.py:101
  197.4 0.0 reduce-scatter.2.cloned.1.call-update
  197.4 0.7 reduce
  198.1 104.7 %all-to-all-done.1 = bf16[32,3,128,512]{3,2,1,0:T(8,128)(2,1)} async-done(((bf16[32,3,128,512]{3,2,1,0:T(8,128)(2,1)}), bf16[32,3,128,512]{3,2,1,0:T(8,128)(2,1)}, u32[]{:S(2)}, u32[]{:S(2)}) %all-to-all-start.1) | async-done | bytes 12582944 | tf_op jit(solution)/shard_map/all_to_all | solution.py:61
  302.8 3.4 broadcast_in_dim.41
  306.3 35.2 %scatter_fusion.3 = bf16[16,3,128,512]{3,2,1,0:T(8,128)(2,1)} fusion(bf16[16,3,128,512]{3,2,1,0:T(8,128)(2,1)} %broadcast_in_dim.41, s32[32]{0:T(128)S(1)} %fusion.41, bf16[32,3,128,512]{3,2,1,0:T(8,128)(2,1)} %all-to-all-done.1), kind=kCustom, calls=%fused_computation.4 | custom fusion | bytes 37748864 | tf_op jit(solution)/shard_map/scatter | solution.py:65
  341.5 0.0 copy-done.5
  341.5 2.5 add_convert_fusion
  (26 shorter events, 0.2 us)
Async XLA Ops:
  7.2 184.4 %copy-start = (bf16[512,2048]{1,0:T(8,128)(2,1)S(1)}, bf16[512,2048]{1,0:T(8,128)(2,1)}, u32[]{:S(2)}) copy-start(bf16[512,2048]{1,0:T(8,128)(2,1)} %param.18) | copy-start | bytes 6291460
  7.2 72.6 %all-gather.2.cloned.1.call-start = ((), (), s32[]{:S(2)}) async-start(), calls=%async_computation.3 | async-start | bytes 5242880 | tf_op jit(solution)/shard_map/all_gather | solution.py:75
  11.4 123.6 %all-to-all-start = ((s32[32,1,1]{2,1,0:T(1,128)}), s32[32,1,1]{2,1,0:T(1,128)S(1)}, u32[]{:S(2)}, u32[]{:S(2)}) async-start(s32[32,1,1]{2,1,0:T(1,128)} %copy.59), calls=%async_computation.1 | async-start | bytes 32768 | tf_op jit(solution)/shard_map/all_to_all | solution.py:62
  68.7 14.6 %copy-start.7 = (f32[2048]{0:T(1024)S(1)}, f32[2048]{0:T(1024)}, u32[]{:S(2)}) copy-start(f32[2048]{0:T(1024)} %param.15) | copy-start | bytes 24580
  68.7 14.6 %copy-start.8 = (f32[2048]{0:T(1024)S(1)}, f32[2048]{0:T(1024)}, u32[]{:S(2)}) copy-start(f32[2048]{0:T(1024)} %param.14) | copy-start | bytes 24580
  68.7 14.6 %copy-start.9 = (f32[1536]{0:T(1024)S(1)}, f32[1536]{0:T(1024)}, u32[]{:S(2)}) copy-start(f32[1536]{0:T(1024)} %param.17) | copy-start | bytes 18436
  103.3 4.6 %copy-start.2 = (f32[1024,3,4,128]{3,2,1,0:T(4,128)S(1)}, f32[1024,3,4,128]{3,2,1,0:T(4,128)}, u32[]{:S(2)}) copy-start(f32[1024,3,4,128]{3,2,1,0:T(4,128)} %reshape.103) | copy-start | bytes 18874372
  107.9 1.2 copy-start.3
  108.5 7.7 %copy-start.4 = (bf16[1024,3,4,128]{3,0,2,1:T(8,128)(2,1)}, bf16[1024,3,4,128]{3,0,2,1:T(8,128)(2,1)S(1)}, u32[]{:S(2)}) copy-start(bf16[1024,3,4,128]{3,0,2,1:T(8,128)(2,1)S(1)} %copy.69) | copy-start | bytes 9437188
  135.0 167.8 %all-to-all-start.1 = ((bf16[32,3,128,512]{3,2,1,0:T(8,128)(2,1)}), bf16[32,3,128,512]{3,2,1,0:T(8,128)(2,1)}, u32[]{:S(2)}, u32[]{:S(2)}) async-start(bf16[32,3,128,512]{3,2,1,0:T(8,128)(2,1)} %scatter_fusion.2), calls=%async_computation.2 | async-start | bytes 25165824 | tf_op jit(solution)/shard_map/all_to_all | solution.py:61
  142.5 199.0 %reduce-scatter.2.cloned.1.call-start = ((), (), s32[]{:S(2)}) async-start(), calls=%async_computation.4 | async-start | bytes 5242880 | tf_op jit(solution)/shard_map/reduce_scatter | solution.py:107
  145.9 3.3 copy-start.1
  162.3 3.3 copy-start.1
  178.6 3.3 copy-start.1
  306.3 35.2 %copy-start.5 = (bf16[1024,512]{1,0:T(8,128)(2,1)S(1)}, bf16[1024,512]{1,0:T(8,128)(2,1)}, u32[]{:S(2)}) copy-start(bf16[1024,512]{1,0:T(8,128)(2,1)} %param.13) | copy-start | bytes 3145732
  306.3 35.2 %copy-start.6 = (f32[512]{0:T(512)S(1)}, f32[512]{0:T(512)}, u32[]{:S(2)}) copy-start(f32[512]{0:T(512)} %param.19) | copy-start | bytes 6148
Sparse Core Ops, SparseCore 0:
  9.6 50.6 all-gather.1
  197.5 63.9 reduce-scatter.1
where the time goes:
time: 353 us; the launch traced here: 351 us
  local copies, waits for them, and re-layouts  122 us (35%)
  waiting for transfers between devices  105 us (30%)
  matrix products  66.9 us (19%)
  other arithmetic  25.3 us (7%)
  starting transfers between devices  15.9 us (5%)
  between operations  14.8 us (4%)
    all_to_all x1, waiting for transfers between devices, move_pages(): lax.all_to_all(outgoing, 'grp', split_axis=0, concat_axis=0, tiled=True)  105 us
    scatter x1, local copies, waits for them, and re-layouts, move_pages(): placed = placed.at[arrived_labels].set(arrived, mode='drop')  35.2 us
    dot_general x4, matrix products, block_update(): jnp.einsum('hck,khd->hcd', expo.astype(jnp.bfloat16), value_block, prefer...  33.4 us
    scatter x2, local copies, waits for them, and re-layouts, move_pages(): outgoing = outgoing.at[target].set(halves[:, :, :, parity, :])  19.7 us
    unnamed x20, local copies, waits for them, and re-layouts  16.7 us
    squeeze x3, local copies, waits for them, and re-layouts, move_pages(): outgoing = outgoing.at[target].set(halves[:, :, :, parity, :])  15.6 us
    dot_general x4, matrix products, block_update(): jnp.einsum('chd,khd->hck', queries, key_block, preferred_element_type=jnp...  15.4 us
    reduce_sum x4, other arithmetic, block_update(): totals = totals * factor + jnp.sum(expo, axis=2)  14.1 us
  transfers between devices with their start and end apart: 4, of which 1 were waited for; matrix products, arithmetic and copies ran while one was open for 57% of the time, Pallas kernels for 0%

commit v1 on v0

v1 whole, which is shorter than its diff:
```python
import functools

import jax
import jax.numpy as jnp
from jax import lax
from jax.experimental import pallas as pl
from jax.experimental.pallas import tpu as pltpu
from jax.sharding import PartitionSpec as P

HEADS = 16
ROWS = 256
WIDE = 1024


NEG = -1e30
EPS = 1e-05

MESH = pl.DeviceIdType.MESH
ANY = pl.BlockSpec(memory_space=pl.ANY)
VMEM = pl.BlockSpec(memory_space=pltpu.VMEM)
SMEM = pl.BlockSpec(memory_space=pltpu.SMEM)


def swap_kernel(
    groups, table_ref, pages_ref, half_ref, tables_ref, own_sem, sent_sem, got_sem, page_out, page_in
):
    me = lax.axis_index("grp")
    core = lax.rem(me, 2)
    partner = me + 1 - 2 * core
    half_width = half_ref.shape[-1]
    page_count = pages_ref.shape[0]

    barrier = pltpu.get_barrier_semaphore()

    def greet(step, none):
        peer = lax.rem(me + step, groups)
        pl.semaphore_signal(barrier, inc=1, device_id={"grp": peer}, device_id_type=MESH)
        return none

    lax.fori_loop(1, groups, greet, 0)
    own = pltpu.make_async_copy(table_ref, tables_ref.at[me], own_sem)
    own.start()
    pl.semaphore_wait(barrier, groups - 1)

    columns = pl.ds(pl.multiple_of((1 - core) * half_width, half_width), half_width)

    def page_copy(number):
        return pltpu.make_async_remote_copy(
            src_ref=pages_ref.at[number, :, :, columns],
            dst_ref=half_ref.at[number],
            send_sem=page_out.at[number],
            recv_sem=page_in.at[number],
            device_id={"grp": partner},
            device_id_type=MESH,
        )

    def table_copy(step):
        return pltpu.make_async_remote_copy(
            src_ref=table_ref,
            dst_ref=tables_ref.at[me],
            send_sem=sent_sem.at[step],
            recv_sem=got_sem.at[step],
            device_id={"grp": lax.rem(me + step, groups)},
            device_id_type=MESH,
        )

    def start_table(step, none):
        table_copy(step).start()
        return none

    def wait_table(step, none):
        table_copy(step).wait()
        return none

    lax.fori_loop(1, groups, start_table, 0)
    for number in range(page_count):
        page_copy(number).start()
    lax.fori_loop(1, groups, wait_table, 0)
    for number in range(page_count):
        page_copy(number).wait()
    own.wait()


def swap_halves(page_table, kv_pages):
    groups = lax.axis_size("grp")
    page_count, layers, page_len, width = kv_pages.shape
    return pl.pallas_call(
        functools.partial(swap_kernel, groups),
        name="swap_halves",
        out_shape=(
            jax.ShapeDtypeStruct((page_count, layers, page_len, width // 2), kv_pages.dtype),
            jax.ShapeDtypeStruct((groups,) + page_table.shape, page_table.dtype),
        ),
        in_specs=[ANY, ANY],
        out_specs=(ANY, ANY),
        scratch_shapes=[
            pltpu.SemaphoreType.DMA,
            pltpu.SemaphoreType.DMA((groups,)),
            pltpu.SemaphoreType.DMA((groups,)),
            pltpu.SemaphoreType.DMA((page_count,)),
            pltpu.SemaphoreType.DMA((page_count,)),
        ],
        compiler_params=pltpu.CompilerParams(collective_id=1, has_side_effects=True),
    )(page_table, kv_pages)


def sort_kernel(source_ref, pages_ref, half_ref, sorted_ref, held, in_sem, out_sem):
    core = lax.rem(lax.axis_index("grp"), 2)
    half_width = half_ref.shape[-1]
    page_count = pages_ref.shape[0]
    columns = pl.ds(pl.multiple_of(core * half_width, half_width), half_width)
    count = sorted_ref.shape[0]

    for slot in range(count):
        source = source_ref[slot]

        @pl.when(source < page_count)
        def _():
            pltpu.make_async_copy(
                pages_ref.at[source, :, :, columns], held.at[slot], in_sem.at[slot]
            ).start()

        @pl.when(source >= page_count)
        def _():
            pltpu.make_async_copy(
                half_ref.at[source - page_count], held.at[slot], in_sem.at[slot]
            ).start()

    outs = []
    for slot in range(count):
        pltpu.make_async_copy(half_ref.at[0], held.at[slot], in_sem.at[slot]).wait()
        out = pltpu.make_async_copy(held.at[slot], sorted_ref.at[slot], out_sem.at[slot])
        out.start()
        outs.append(out)
    for out in outs:
        out.wait()


def sort_pages(source, kv_pages, half, count):
    shape = (count,) + half.shape[1:]
    return pl.pallas_call(
        sort_kernel,
        name="sort_pages",
        out_shape=jax.ShapeDtypeStruct(shape, half.dtype),
        in_specs=[SMEM, ANY, ANY],
        out_specs=ANY,
        scratch_shapes=[
            pltpu.VMEM(shape, half.dtype),
            pltpu.SemaphoreType.DMA((count,)),
            pltpu.SemaphoreType.DMA((count,)),
        ],
    )(source, kv_pages, half)


def place_kernel(rounds, *refs):
    slots = refs[:rounds]
    valids = refs[rounds : 2 * rounds]
    arrived = refs[2 * rounds : 3 * rounds]
    placed_ref, held, in_sem, out_sem = refs[3 * rounds :]
    count = arrived[0].shape[0]
    for number in range(rounds):
        for chip in range(count):
            pltpu.make_async_copy(
                arrived[number].at[chip], held.at[chip], in_sem.at[chip]
            ).start()
        for chip in range(count):
            pltpu.make_async_copy(
                arrived[number].at[chip], held.at[chip], in_sem.at[chip]
            ).wait()

            @pl.when(valids[number][chip] > 0)
            def _():
                pltpu.make_async_copy(
                    held.at[chip], placed_ref.at[0, slots[number][chip]], out_sem.at[chip]
                ).start()

        for chip in range(count):

            @pl.when(valids[number][chip] > 0)
            def _():
                pltpu.make_async_copy(
                    held.at[chip], placed_ref.at[0, slots[number][chip]], out_sem.at[chip]
                ).wait()


def place_pages(slots, valids, arrived):
    rounds = len(arrived)
    count = arrived[0].shape[0]
    return pl.pallas_call(
        functools.partial(place_kernel, rounds),
        name="place_pages",
        out_shape=jax.ShapeDtypeStruct((1,) + arrived[0].shape, arrived[0].dtype),
        in_specs=[SMEM] * (2 * rounds) + [ANY] * rounds,
        out_specs=ANY,
        scratch_shapes=[
            pltpu.VMEM(arrived[0].shape, arrived[0].dtype),
            pltpu.SemaphoreType.DMA((count,)),
            pltpu.SemaphoreType.DMA((count,)),
        ],
    )(*slots, *valids, *arrived)


def move_pages(kv_pages, page_table):
    groups = lax.axis_size("grp")
    chips = groups // 2
    page_count = kv_pages.shape[0]
    half, tables = swap_halves(page_table, kv_pages)
    wanted = tables[:, :, 0].reshape(chips, 2 * page_count)
    slot_ids = tables[:, :, 1].reshape(chips, 2 * page_count)
    me = lax.axis_index("grp")
    chip = me // 2
    core = me % 2
    order = jnp.arange(2 * page_count)
    again = jnp.any(
        (wanted[:, :, None] == wanted[:, None, :]) & (order[None, :, None] > order[None, None, :]),
        axis=2,
    )
    own = lax.dynamic_index_in_dim(wanted, chip, 0, keepdims=False)
    own_again = lax.dynamic_index_in_dim(again, chip, 0, keepdims=False)
    local = (order + 2 * page_count - page_count * core) % (2 * page_count)

    def source_of(number):
        fits = (own[None, :] == jnp.arange(chips)[:, None]) & (own_again == (number > 0))[None, :]
        return jnp.sum(jnp.where(fits, local[None, :], 0), axis=1).astype(jnp.int32)

    def labels_of(number):
        fits = (wanted == chip) & (again == (number > 0))
        slot = jnp.sum(jnp.where(fits, slot_ids, 0), axis=1).astype(jnp.int32)
        return slot, jnp.any(fits, axis=1).astype(jnp.int32)

    across = [list(range(0, groups, 2)), list(range(1, groups, 2))]

    def exchange(number):
        outgoing = sort_pages(source_of(number), kv_pages, half, chips)
        return lax.all_to_all(
            outgoing, "grp", split_axis=0, concat_axis=0, tiled=True, axis_index_groups=across
        )

    first = exchange(0)
    slot, valid = labels_of(0)

    def finish():
        def twice(arrived):
            second = exchange(1)
            slot2, valid2 = labels_of(1)
            return place_pages((slot, slot2), (valid, valid2), (arrived, second))

        def once(arrived):
            return place_pages((slot,), (valid,), (arrived,))

        return lax.cond(jnp.any(again), twice, once, first)

    return finish


def flash(state, queries, keys, values, allowed):
    scores = lax.dot_general(
        queries, keys, (((1,), (1,)), ((), ())), preferred_element_type=jnp.float32
    )
    if allowed is not None:
        scores = jnp.where(allowed, scores, NEG)
    top = jnp.max(scores, axis=1, keepdims=True)
    if state is None:
        raised = top
    else:
        highest, totals, running = state
        raised = jnp.maximum(highest, top)
    expo = jnp.exp(scores - raised)
    sums = jnp.sum(expo, axis=1, keepdims=True)
    part = jnp.dot(expo.astype(jnp.bfloat16), values, preferred_element_type=jnp.float32)
    if state is None:
        return raised, sums, part
    factor = jnp.exp(highest - raised)
    return raised, totals * factor + sums, running * factor + part


def block_kernel(
    tp,
    head_count,
    tokens_ref,
    gain_ref,
    bias_ref,
    w_qkv_ref,
    b_qkv_ref,
    w_out_ref,
    b_out_ref,
    cache_ref,
    length_ref,
    mixed_ref,
    whole,
    w_qkv,
    w_out,
    cache,
    normed,
    qkv,
    attended,
    terms,
    got,
    mix,
    load_sem,
    tok_out,
    tok_in,
    term_out,
    term_in,
):
    me = lax.axis_index("tp")
    rows_all, width = tokens_ref.shape
    chunks = rows_all // ROWS
    features = tp * width
    size = w_out_ref.shape[0] // head_count
    part_width = head_count * size
    prefix = cache_ref.shape[0]

    loads = [
        pltpu.make_async_copy(tokens_ref, whole.at[me], load_sem.at[0]),
        pltpu.make_async_copy(w_qkv_ref, w_qkv, load_sem.at[1]),
        pltpu.make_async_copy(cache_ref, cache, load_sem.at[2]),
        pltpu.make_async_copy(w_out_ref, w_out, load_sem.at[3]),
    ]
    for load in loads:
        load.start()

    barrier = pltpu.get_barrier_semaphore()
    for step in range(1, tp):
        pl.semaphore_signal(
            barrier, inc=1, device_id={"tp": lax.rem(me + step, tp)}, device_id_type=MESH
        )
    pl.semaphore_wait(barrier, tp - 1)

    def rows_of(chunk):
        return pl.ds(pl.multiple_of(chunk * ROWS, ROWS), ROWS)

    def token_copy(chunk, step):
        rows = rows_of(chunk)
        return pltpu.make_async_remote_copy(
            src_ref=tokens_ref.at[rows],
            dst_ref=whole.at[me, rows],
            send_sem=tok_out.at[chunk, step],
            recv_sem=tok_in.at[chunk, step],
            device_id={"tp": lax.rem(me + step, tp)},
            device_id_type=MESH,
        )

    def term_copy(chunk, step):
        rows = rows_of(chunk)
        return pltpu.make_async_remote_copy(
            src_ref=terms.at[step, rows],
            dst_ref=got.at[step, rows],
            send_sem=term_out.at[chunk, step],
            recv_sem=term_in.at[chunk, step],
            device_id={"tp": lax.rem(me + step, tp)},
            device_id_type=MESH,
        )

    order = (2, 1, 3)
    for chunk in range(chunks):
        for step in order:
            token_copy(chunk, step).start()
    for load in loads:
        load.wait()

    length = length_ref[lax.axis_index("grp")]

    def finish(chunk):
        rows = rows_of(chunk)
        total = mix[rows, :]
        for step in order:
            term_copy(chunk, step).wait_recv()
            total += got[step, rows, :].astype(jnp.float32)
        mixed_ref[rows, :] = total.astype(jnp.bfloat16)

    def visit(chunk, none):
        rows = rows_of(chunk)
        for step in order:
            token_copy(chunk, step).wait_recv()
        sums = jnp.zeros((ROWS, 1), jnp.float32)
        squares = jnp.zeros((ROWS, 1), jnp.float32)
        for peer in range(tp):
            piece = whole[peer, rows, :].astype(jnp.float32)
            sums += jnp.sum(piece, axis=1, keepdims=True)
            squares += jnp.sum(piece * piece, axis=1, keepdims=True)
        center = sums * (1.0 / features)
        spread = squares * (1.0 / features) - center * center
        scale = lax.rsqrt(spread + EPS)
        for peer in range(tp):
            columns = pl.ds(peer * width, width)
            piece = whole[peer, rows, :].astype(jnp.float32)
            normed[:, columns] = (
                (piece - center) * scale * gain_ref[:, columns] + bias_ref[:, columns]
            ).astype(jnp.bfloat16)
        for part in range(3):
            columns = pl.ds(part * part_width, part_width)
            projected = (
                jnp.dot(normed[...], w_qkv[:, columns], preferred_element_type=jnp.float32)
                + b_qkv_ref[:, columns]
            )
            if part == 0:
                projected = projected * size ** (-0.5)
            qkv[rows, columns] = projected.astype(jnp.bfloat16)

        def head(number, none):
            def lanes(start):
                return pl.ds(pl.multiple_of(start, size), size)

            queries = qkv[rows, lanes(number * size)]
            state = None
            for block in range(prefix // WIDE):
                base = block * WIDE
                keys = cache[pl.ds(base, WIDE), lanes(number * 2 * size)]
                values = cache[pl.ds(base, WIDE), lanes(number * 2 * size + size)]
                position = base + lax.broadcasted_iota(jnp.int32, (1, WIDE), 1)
                state = flash(state, queries, keys, values, position < length)

            def earlier(other, state):
                keys = qkv[rows_of(other), lanes(part_width + number * size)]
                values = qkv[rows_of(other), lanes(2 * part_width + number * size)]
                return flash(state, queries, keys, values, None)

            state = lax.fori_loop(0, chunk, earlier, state)
            keys = qkv[rows, lanes(part_width + number * size)]
            values = qkv[rows, lanes(2 * part_width + number * size)]
            causal = lax.broadcasted_iota(jnp.int32, (ROWS, ROWS), 1) <= lax.broadcasted_iota(
                jnp.int32, (ROWS, ROWS), 0
            )
            highest, totals, running = flash(state, queries, keys, values, causal)
            attended[:, lanes(number * size)] = (running / totals).astype(jnp.bfloat16)
            return none

        lax.fori_loop(0, head_count, head, 0)

        def term(step):
            columns = pl.ds(pl.multiple_of(lax.rem(me + step, tp) * width, width), width)
            return jnp.dot(attended[...], w_out[:, columns], preferred_element_type=jnp.float32)

        for step in order:
            terms[step, rows, :] = term(step).astype(jnp.bfloat16)
            term_copy(chunk, step).start()
        mix[rows, :] = term(0) + whole[me, rows, :].astype(jnp.float32) + b_out_ref[...]

        @pl.when(chunk > 0)
        def _():
            finish(chunk - 1)

        return none

    lax.fori_loop(0, chunks, visit, 0)
    finish(chunks - 1)
    for chunk in range(chunks):
        for step in order:
            token_copy(chunk, step).wait_send()
            term_copy(chunk, step).wait_send()


def block(tokens, ln_gain, ln_bias, w_qkv, b_qkv, w_out, b_out, kv_cache, prefix_len):
    tp = lax.axis_size("tp")
    rows, width = tokens.shape
    head_count = HEADS // tp
    chunks = rows // ROWS
    bf16 = jnp.bfloat16
    return pl.pallas_call(
        functools.partial(block_kernel, tp, head_count),
        name="block",
        out_shape=jax.ShapeDtypeStruct((rows, width), bf16),
        in_specs=[ANY, VMEM, VMEM, ANY, VMEM, ANY, VMEM, ANY, SMEM],
        out_specs=VMEM,
        scratch_shapes=[
            pltpu.VMEM((tp, rows, width), bf16),
            pltpu.VMEM(w_qkv.shape, bf16),
            pltpu.VMEM(w_out.shape, bf16),
            pltpu.VMEM(kv_cache.shape, bf16),
            pltpu.VMEM((ROWS, tp * width), bf16),
            pltpu.VMEM((rows, w_qkv.shape[1]), bf16),
            pltpu.VMEM((ROWS, w_out.shape[0]), bf16),
            pltpu.VMEM((tp, rows, width), bf16),
            pltpu.VMEM((tp, rows, width), bf16),
            pltpu.VMEM((rows, width), jnp.float32),
            pltpu.SemaphoreType.DMA((4,)),
            pltpu.SemaphoreType.DMA((chunks, tp)),
            pltpu.SemaphoreType.DMA((chunks, tp)),
            pltpu.SemaphoreType.DMA((chunks, tp)),
            pltpu.SemaphoreType.DMA((chunks, tp)),
        ],
        cost_estimate=pl.CostEstimate(
            flops=40_000_000_000, bytes_accessed=20_000_000, transcendentals=0
        ),
        compiler_params=pltpu.CompilerParams(
            collective_id=0, has_side_effects=True, vmem_limit_bytes=56 << 20
        ),
    )(
        tokens,
        ln_gain[None],
        ln_bias[None],
        w_qkv,
        b_qkv[None],
        w_out,
        b_out[None],
        kv_cache,
        prefix_len,
    )


def shards(
    tokens, ln_gain, ln_bias, w_qkv, b_qkv, w_out, b_out, kv_cache, prefix_len, kv_pages, page_table
):
    finish = move_pages(kv_pages, page_table)
    mixed = block(tokens, ln_gain, ln_bias, w_qkv, b_qkv, w_out, b_out, kv_cache, prefix_len)
    return (mixed, finish())


def solution(mesh):
    placed = (
        P("grp", "tp"),
        P(),
        P(),
        P(None, "tp"),
        P("tp"),
        P("tp", None),
        P("tp"),
        P("grp", "tp"),
        P(),
        P("grp", None, None, "tp"),
        P("grp", None),
    )
    return jax.shard_map(
        shards,
        mesh=mesh,
        in_specs=placed,
        out_specs=(P("grp", "tp"), P("grp", None, None, None, "tp")),
        check_vma=False,
    )
```

time: 353 us -> 147 us (0.42)
  the two profiles are of different devices: /device:TPU:0 before, /device:TPU:14 now
where the time goes in v1:
time: 147 us; the launch traced here: 145 us
  Pallas kernels  128 us (87%)
  local copies, waits for them, and re-layouts  6.11 us (4%)
  starting transfers between devices  5.85 us (4%)
  other arithmetic  3.37 us (2%)
    pallas_call x1, Pallas kernels, block(): pl.pallas_call(functools.partial(block_kernel, tp, head_count), name='blo...  104 us
    pallas_call x1, Pallas kernels, swap_halves(): pl.pallas_call(functools.partial(swap_kernel, groups), name='swap_halves'...  12.2 us
    pallas_call x1, Pallas kernels, place_pages(): pl.pallas_call(functools.partial(place_kernel, rounds), name='place_pages...  6.03 us
    all_to_all x1, starting transfers between devices, exchange(): lax.all_to_all(outgoing, 'grp', split_axis=0, concat_axis=0, tiled=True,...  5.85 us
    pallas_call x1, Pallas kernels, sort_pages(): pl.pallas_call(sort_kernel, name='sort_pages', out_shape=jax.ShapeDtypeSt...  5.21 us
    unnamed x6, local copies, waits for them, and re-layouts  3.62 us
  transfers between devices with their start and end apart: 1, of which 0 were waited for; matrix products, arithmetic and copies ran while one was open for 2% of the time, Pallas kernels for 72%

profile of v1, /device:TPU:14, one launch (start us, length us, event | category | flops | bytes accessed | tf_op | source)
XLA Modules:
  0.0 144.7 jit_solution(14666157558594426052)
XLA Ops:
  0.7 1.3 copy.18.table_ref
  2.0 12.2 %swap_halves.1 = (bf16[8,3,128,512]{3,2,1,0:T(8,128)(2,1)S(1)}, s32[32,8,2]{2,1,0:T(8,128)}) custom-call(s32[8,2]{1,0:T(8,128)} %copy.18.table_ref, bf16[8,3,128,1024]{3,2,1,0:T(8,128)(2,1)} %pages_ref.3), custom_call_target="tpu_custom_call" | custom-call | tf_op jit(solution)/shard_map/swap_halves/pallas_call | solution.py:87
  14.2 1.5 %slice_reduce_fusion = s32[32,8]{1,0:T(8,128)S(1)} fusion(s32[32,8,2]{2,1,0:T(8,128)} %get-tuple-element.68), kind=kLoop, calls=%fused_computation.11 | loop fusion | bytes 2048 | tf_op jit(solution)/shard_map/slice | solution.py:208
  15.7 0.1 eq.82
  15.8 1.0 fusion.1
  16.8 0.7 select_reduce_fusion.3.source_ref
  17.5 5.2 %sort_pages.3 = bf16[16,3,128,512]{3,2,1,0:T(8,128)(2,1)} custom-call(s32[16]{0:T(128)} %select_reduce_fusion.3.source_ref, bf16[8,3,128,1024]{3,2,1,0:T(8,128)(2,1)} %pages_ref.3, bf16[8,3,128,512]{3,2,1,0:T(8,128)(2,1)S(1)} %get-tuple-element.69.half_ref), custom_call_target="tpu_custom_call" | custom-call | tf_op jit(solution)/shard_map/sort_pages/pallas_call | solution.py:141
  22.7 0.0 copy-start
  22.7 0.0 copy-start.1
  22.8 5.9 %all-to-all-start.1 = ((bf16[16,3,128,512]{3,2,1,0:T(8,128)(2,1)}), bf16[16,3,128,512]{3,2,1,0:T(8,128)(2,1)}, u32[]{:S(2)}, u32[]{:S(2)}) async-start(bf16[16,3,128,512]{3,2,1,0:T(8,128)(2,1)} %sort_pages.3), calls=%async_computation.1 | async-start | bytes 12582912 | tf_op jit(solution)/shard_map/all_to_all | solution.py:235
  28.6 0.1 eq.96
  28.7 0.0 copy-done
  28.8 0.7 fusion.6
  29.4 0.7 fusion.7
  30.2 0.1 reduce_sum.44
  30.2 0.1 reduce_sum.45
  30.4 0.1 reduce_or.46
  30.5 0.1 reduce_or.47
  31.3 0.0 copy-done.1
  31.3 0.6 broadcast_in_dim.49.b_qkv_ref
  31.9 104.4 %block.1 = bf16[1024,512]{1,0:T(8,128)(2,1)} custom-call(bf16[1024,512]{1,0:T(8,128)(2,1)} %tokens_ref.1, f32[1,2048]{1,0:T(1,128)} %bitcast.9, f32[1,2048]{1,0:T(1,128)} %bitcast.10, bf16[2048,1536]{1,0:T(8,128)(2,1)} %w_qkv_ref.1, f32[1,1536]{1,0:T(1,128)} %broadcast_in_dim.49.b_qkv_ref, bf16[512,2048]{1,0:T(8,128)(2,1)} %w_out_ref.1, f32[1,512]{1,0:T(1,128)} %bitcast.11, ...), custom_call_target="tpu_custom_call" | custom-call | flops 40000000000 | bytes 20000000 | tf_op jit(solution)/shard_map/block/pallas_call | solution.py:460
  136.3 0.0 all-to-all-done.1
  136.3 6.0 %conditional.1 = (bf16[1,16,3,128,512]{4,3,2,1,0:T(8,128)(2,1)}) conditional(s32[]{:T(128)} %convert_element_type.9, (s32[16]{0:T(128)S(1)}, s32[16]{0:T(128)S(1)}, bf16[16,3,128,512]{3,2,1,0:T(8,128)(2,1)}) %tuple.15, (s32[]{:T(128)}, s32[16,16]{1,0:T(8,128)S(1)}, pred[16,16]{1,0:T(8,128)(4,1)S(1)}, s32[32,8,1]{2,1,0:T(8,128)S(1)}, ...), branch_computations={%region_7.8_spmd, %region_8.12_spmd} | conditional | flops 2352 | bytes 18881888 | solution.py:251
  136.4 6.0 %place_pages.2 = bf16[1,16,3,128,512]{4,3,2,1,0:T(8,128)(2,1)} custom-call(s32[16]{0:T(128)S(1)} %get-tuple-element.48.refs_0_, s32[16]{0:T(128)S(1)} %get-tuple-element.49.refs_1_, bf16[16,3,128,512]{3,2,1,0:T(8,128)(2,1)} %get-tuple-element.50.refs_2_), custom_call_target="tpu_custom_call" | custom-call | tf_op jit(solution)/shard_map/cond/branch_0_fun/place_pages/pallas_call | solution.py:189
  142.4 2.3 %copy.24 = bf16[1024,512]{1,0:T(8,128)(2,1)} copy(bf16[1024,512]{1,0:T(8,128)(2,1)} %block.1) | data formatting | bytes 2097152
  (8 shorter events, 0.1 us)
Async XLA Ops:
  22.7 6.0 %copy-start = (s32[32,8,2]{2,1,0:T(8,128)S(1)}, s32[32,8,2]{2,1,0:T(8,128)}, u32[]{:S(2)}) copy-start(s32[32,8,2]{2,1,0:T(8,128)} %get-tuple-element.68) | copy-start | bytes 6148
  22.7 8.5 %copy-start.1 = (f32[1536]{0:T(1024)S(1)}, f32[1536]{0:T(1024)}, u32[]{:S(2)}) copy-start(f32[1536]{0:T(1024)} %param.17) | copy-start | bytes 18436
  22.8 113.6 %all-to-all-start.1 = ((bf16[16,3,128,512]{3,2,1,0:T(8,128)(2,1)}), bf16[16,3,128,512]{3,2,1,0:T(8,128)(2,1)}, u32[]{:S(2)}, u32[]{:S(2)}) async-start(bf16[16,3,128,512]{3,2,1,0:T(8,128)(2,1)} %sort_pages.3), calls=%async_computation.1 | async-start | bytes 12582912 | tf_op jit(solution)/shard_map/all_to_all | solution.py:235

commit v2 on v1

--- a/solution.py
+++ b/solution.py
@@ -9,6 +9,7 @@
 
 HEADS = 16
 ROWS = 256
+PAGE_ORDER = (4, 1, 12, 3, 5, 15, 7, 13, 8, 2, 9, 6, 11, 14, 10)
 WIDE = 1024
 
 
@@ -200,57 +201,46 @@
     )(*slots, *valids, *arrived)
 
 
-def move_pages(kv_pages, page_table):
+def again_in(tables):
+    chips = tables.shape[0] // 2
+    wanted = tables[:, 0, :].reshape(chips, -1)
+    order = jnp.arange(wanted.shape[1])
+    return jnp.any(
+        (wanted[:, :, None] == wanted[:, None, :]) & (order[None, :, None] > order[None, None, :]),
+        axis=2,
+    )
+
+
+def move_twice(kv_pages, page_table):
     groups = lax.axis_size("grp")
     chips = groups // 2
     page_count = kv_pages.shape[0]
-    half, tables = swap_halves(page_table, kv_pages)
-    wanted = tables[:, :, 0].reshape(chips, 2 * page_count)
-    slot_ids = tables[:, :, 1].reshape(chips, 2 * page_count)
+    half, tables = swap_halves(page_table.T, kv_pages)
+    again = again_in(tables)
+    wanted = tables[:, 0, :].reshape(chips, -1)
+    slot_ids = tables[:, 1, :].reshape(chips, -1)
     me = lax.axis_index("grp")
     chip = me // 2
     core = me % 2
     order = jnp.arange(2 * page_count)
-    again = jnp.any(
-        (wanted[:, :, None] == wanted[:, None, :]) & (order[None, :, None] > order[None, None, :]),
-        axis=2,
-    )
     own = lax.dynamic_index_in_dim(wanted, chip, 0, keepdims=False)
     own_again = lax.dynamic_index_in_dim(again, chip, 0, keepdims=False)
     local = (order + 2 * page_count - page_count * core) % (2 * page_count)
-
-    def source_of(number):
+    across = [list(range(0, groups, 2)), list(range(1, groups, 2))]
+    slots, valids, arrived = [], [], []
+    for number in range(2):
         fits = (own[None, :] == jnp.arange(chips)[:, None]) & (own_again == (number > 0))[None, :]
-        return jnp.sum(jnp.where(fits, local[None, :], 0), axis=1).astype(jnp.int32)
-
-    def labels_of(number):
+        source = jnp.sum(jnp.where(fits, local[None, :], 0), axis=1).astype(jnp.int32)
+        outgoing = sort_pages(source, kv_pages, half, chips)
+        arrived.append(
+            lax.all_to_all(
+                outgoing, "grp", split_axis=0, concat_axis=0, tiled=True, axis_index_groups=across
+            )
+        )
         fits = (wanted == chip) & (again == (number > 0))
-        slot = jnp.sum(jnp.where(fits, slot_ids, 0), axis=1).astype(jnp.int32)
-        return slot, jnp.any(fits, axis=1).astype(jnp.int32)
-
-    across = [list(range(0, groups, 2)), list(range(1, groups, 2))]
-
-    def exchange(number):
-        outgoing = sort_pages(source_of(number), kv_pages, half, chips)
-        return lax.all_to_all(
-            outgoing, "grp", split_axis=0, concat_axis=0, tiled=True, axis_index_groups=across
-        )
-
-    first = exchange(0)
-    slot, valid = labels_of(0)
-
-    def finish():
-        def twice(arrived):
-            second = exchange(1)
-            slot2, valid2 = labels_of(1)
-            return place_pages((slot, slot2), (valid, valid2), (arrived, second))
-
-        def once(arrived):
-            return place_pages((slot,), (valid,), (arrived,))
-
-        return lax.cond(jnp.any(again), twice, once, first)
-
-    return finish
+        slots.append(jnp.sum(jnp.where(fits, slot_ids, 0), axis=1).astype(jnp.int32))
+        valids.append(jnp.any(fits, axis=1).astype(jnp.int32))
+    return place_pages(slots, valids, arrived)
 
 
 def flash(state, queries, keys, values, allowed):
@@ -276,6 +266,7 @@
 
 def block_kernel(
     tp,
+    groups,
     head_count,
     tokens_ref,
     gain_ref,
@@ -286,7 +277,11 @@
     b_out_ref,
     cache_ref,
     length_ref,
+    table_ref,
+    pages_ref,
     mixed_ref,
+    placed_ref,
+    tables_ref,
     whole,
     w_qkv,
     w_out,
@@ -300,12 +295,44 @@
     load_sem,
     tok_out,
     tok_in,
-    term_out,
-    term_in,
+    relay_out,
+    relay_in,
+    far_out,
+    far_in,
+    near_out,
+    near_in,
+    pages,
+    ordered,
+    arrived,
+    tables,
+    tables_here,
+    slots,
+    sources,
+    half_load,
+    half_out,
+    half_in,
+    table_load,
+    table_out,
+    table_in,
+    table_save,
+    page_out,
+    page_in,
+    place_out,
 ):
     me = lax.axis_index("tp")
+    group = lax.axis_index("grp")
+    chip = group // 2
+    core = lax.rem(group, 2)
+    partner = group + 1 - 2 * core
+    page_count = pages_ref.shape[0]
+    layers = pages_ref.shape[1]
+    half_width = placed_ref.shape[-1]
+    near_columns = pl.ds(pl.multiple_of(core * half_width, half_width), half_width)
+    far_columns = pl.ds(pl.multiple_of((1 - core) * half_width, half_width), half_width)
     rows_all, width = tokens_ref.shape
     chunks = rows_all // ROWS
+    chips = groups // 2
+    side = 4
     features = tp * width
     size = w_out_ref.shape[0] // head_count
     part_width = head_count * size
@@ -317,62 +344,201 @@
         pltpu.make_async_copy(cache_ref, cache, load_sem.at[2]),
         pltpu.make_async_copy(w_out_ref, w_out, load_sem.at[3]),
     ]
+    loads += [
+        pltpu.make_async_copy(
+            pages_ref.at[number, :, :, near_columns],
+            pages.at[core * page_count + number],
+            half_load.at[number],
+        )
+        for number in range(page_count)
+    ]
+    loads.append(pltpu.make_async_copy(table_ref, tables.at[group], table_load))
     for load in loads:
         load.start()
 
+    sides = (1, 3)
     barrier = pltpu.get_barrier_semaphore()
-    for step in range(1, tp):
+    for step in sides:
         pl.semaphore_signal(
             barrier, inc=1, device_id={"tp": lax.rem(me + step, tp)}, device_id_type=MESH
         )
-    pl.semaphore_wait(barrier, tp - 1)
+
+    def greet(step, none):
+        peer = lax.rem(group + step, groups)
+        pl.semaphore_signal(barrier, inc=1, device_id={"grp": peer}, device_id_type=MESH)
+        return none
+
+    lax.fori_loop(1, groups, greet, 0)
+    pl.semaphore_wait(barrier, groups - 1 + len(sides))
 
     def rows_of(chunk):
         return pl.ds(pl.multiple_of(chunk * ROWS, ROWS), ROWS)
 
-    def token_copy(chunk, step):
-        rows = rows_of(chunk)
+    def half_of(chunk, step):
+        start = chunk * ROWS + (0 if step == 1 else ROWS // 2)
+        return pl.ds(pl.multiple_of(start, ROWS // 2), ROWS // 2)
+
+    def send(src, dst, out_sem, in_sem, step):
         return pltpu.make_async_remote_copy(
-            src_ref=tokens_ref.at[rows],
-            dst_ref=whole.at[me, rows],
-            send_sem=tok_out.at[chunk, step],
-            recv_sem=tok_in.at[chunk, step],
+            src_ref=src,
+            dst_ref=dst,
+            send_sem=out_sem,
+            recv_sem=in_sem,
             device_id={"tp": lax.rem(me + step, tp)},
             device_id_type=MESH,
         )
 
-    def term_copy(chunk, step):
+    def own_copy(chunk, step):
         rows = rows_of(chunk)
+        sems = tok_out.at[chunk, step], tok_in.at[chunk, step]
+        return send(tokens_ref.at[rows], whole.at[me, rows], *sems, step)
+
+    def relay_copy(chunk, step):
+        block = whole.at[lax.rem(me + tp - step, tp), half_of(chunk, step)]
+        return send(block, block, relay_out.at[chunk, step], relay_in.at[chunk, step], step)
+
+    def far_copy(chunk, step):
+        rows = half_of(chunk, step)
+        sems = far_out.at[chunk, step], far_in.at[chunk, step]
+        return send(terms.at[2, rows], got.at[2, rows], *sems, step)
+
+    def near_copy(chunk, step):
+        rows = rows_of(chunk)
+        sems = near_out.at[chunk, step], near_in.at[chunk, step]
+        return send(terms.at[step, rows], got.at[step, rows], *sems, step)
+
+    def relay(chunk):
+        for step in sides:
+            own_copy(chunk, step).wait_recv()
+        for step in sides:
+            relay_copy(chunk, step).start()
+
+    def pass_on(chunk):
+        for step in sides:
+            rows = half_of(chunk, step)
+            far_copy(chunk, step).wait_recv()
+            terms[step, rows, :] = (
+                terms[step, rows, :].astype(jnp.float32) + got[2, rows, :].astype(jnp.float32)
+            ).astype(jnp.bfloat16)
+        for step in sides:
+            near_copy(chunk, step).start()
+
+    def half_copy(number):
         return pltpu.make_async_remote_copy(
-            src_ref=terms.at[step, rows],
-            dst_ref=got.at[step, rows],
-            send_sem=term_out.at[chunk, step],
-            recv_sem=term_in.at[chunk, step],
-            device_id={"tp": lax.rem(me + step, tp)},
+            src_ref=pages_ref.at[number, :, :, far_columns],
+            dst_ref=pages.at[core * page_count + number],
+            send_sem=half_out.at[number],
+            recv_sem=half_in.at[number],
+            device_id={"grp": partner},
             device_id_type=MESH,
         )
 
-    order = (2, 1, 3)
-    for chunk in range(chunks):
-        for step in order:
-            token_copy(chunk, step).start()
+    def table_copy(step):
+        return pltpu.make_async_remote_copy(
+            src_ref=table_ref,
+            dst_ref=tables.at[group],
+            send_sem=table_out.at[step],
+            recv_sem=table_in.at[step],
+            device_id={"grp": lax.rem(group + step, groups)},
+            device_id_type=MESH,
+        )
+
+    def start_table(step, none):
+        table_copy(step).start()
+        return none
+
+    def wait_table(step, none):
+        table_copy(step).wait()
+        return none
+
+    def page_copy(step, layer):
+        down, along = step // side, step % side
+        target = (
+            lax.rem(chip // side + down, side) * side + lax.rem(lax.rem(chip, side) + along, side)
+        )
+        return pltpu.make_async_remote_copy(
+            src_ref=ordered.at[target, layer],
+            dst_ref=arrived.at[chip, layer],
+            send_sem=page_out.at[step, layer],
+            recv_sem=page_in.at[step, layer],
+            device_id={"grp": target * 2 + core},
+            device_id_type=MESH,
+        )
+
+    def request_of(owner, entry):
+        return tables_here[2 * owner + entry // page_count, 0, entry % page_count]
+
+    def first_of(owner, request, value):
+        found = 0
+        for entry in reversed(range(2 * page_count)):
+            found = jnp.where(request_of(owner, entry) == request, value(entry), found)
+        return found
+
+    for step in sides:
+        own_copy(0, step).start()
+    for number in range(page_count):
+        half_copy(number).start()
+    lax.fori_loop(1, groups, start_table, 0)
+    relay(0)
+    for step in sides:
+        own_copy(1, step).start()
     for load in loads:
         load.wait()
+    lax.fori_loop(1, groups, wait_table, 0)
+    saves = [
+        pltpu.make_async_copy(tables, tables_here, table_save.at[0]),
+        pltpu.make_async_copy(tables, tables_ref, table_save.at[1]),
+    ]
+    for save in saves:
+        save.start()
+    for save in saves:
+        save.wait()
+    for number in range(page_count):
+        half_copy(number).wait()
+
+    def order_page(request, none):
+        ordered[request] = pages[first_of(chip, request, lambda entry: entry)]
+        return none
+
+    lax.fori_loop(0, chips, order_page, 0)
+    arrived[chip] = ordered[chip]
+    for layer in range(layers):
+        for step in PAGE_ORDER:
+            page_copy(step, layer).start()
+
+    def slot_from(owner, none):
+        slots[owner] = first_of(
+            owner,
+            chip,
+            lambda entry: tables_here[2 * owner + entry // page_count, 1, entry % page_count],
+        )
+        return none
+
+    lax.fori_loop(0, chips, slot_from, 0)
+
+    def source_to(slot, none):
+        found = 0
+        for owner in range(chips):
+            found = jnp.where(slots[owner] == slot, owner, found)
+        sources[slot] = found
+        return none
+
+    lax.fori_loop(0, chips, source_to, 0)
 
     length = length_ref[lax.axis_index("grp")]
 
     def finish(chunk):
         rows = rows_of(chunk)
         total = mix[rows, :]
-        for step in order:
-            term_copy(chunk, step).wait_recv()
+        for step in sides:
+            near_copy(chunk, step).wait_recv()
             total += got[step, rows, :].astype(jnp.float32)
         mixed_ref[rows, :] = total.astype(jnp.bfloat16)
 
     def visit(chunk, none):
         rows = rows_of(chunk)
-        for step in order:
-            token_copy(chunk, step).wait_recv()
+        for step in sides:
+            relay_copy(chunk, step).wait_recv()
         sums = jnp.zeros((ROWS, 1), jnp.float32)
         squares = jnp.zeros((ROWS, 1), jnp.float32)
         for peer in range(tp):
@@ -402,6 +568,21 @@
             def lanes(start):
                 return pl.ds(pl.multiple_of(start, size), size)
 
+            @pl.when((number == 0) & (chunk + 1 < chunks))
+            def _():
+                relay(chunk + 1)
+
+            @pl.when((number == 0) & (chunk > 0))
+            def _():
+                pass_on(chunk - 1)
+
+            for later in range(2, chunks):
+
+                @pl.when((chunk == 0) & (number == 2 * (later - 2)))
+                def _():
+                    for step in sides:
+                        own_copy(later, step).start()
+
             queries = qkv[rows, lanes(number * size)]
             state = None
             for block in range(prefix // WIDE):
@@ -432,9 +613,11 @@
             columns = pl.ds(pl.multiple_of(lax.rem(me + step, tp) * width, width), width)
             return jnp.dot(attended[...], w_out[:, columns], preferred_element_type=jnp.float32)
 
-        for step in order:
+        terms[2, rows, :] = term(2).astype(jnp.bfloat16)
+        for step in sides:
+            far_copy(chunk, step).start()
+        for step in sides:
             terms[step, rows, :] = term(step).astype(jnp.bfloat16)
-            term_copy(chunk, step).start()
         mix[rows, :] = term(0) + whole[me, rows, :].astype(jnp.float32) + b_out_ref[...]
 
         @pl.when(chunk > 0)
@@ -444,25 +627,56 @@
         return none
 
     lax.fori_loop(0, chunks, visit, 0)
+    pass_on(chunks - 1)
     finish(chunks - 1)
     for chunk in range(chunks):
-        for step in order:
-            token_copy(chunk, step).wait_send()
-            term_copy(chunk, step).wait_send()
-
-
-def block(tokens, ln_gain, ln_bias, w_qkv, b_qkv, w_out, b_out, kv_cache, prefix_len):
+        for step in sides:
+            own_copy(chunk, step).wait_send()
+            relay_copy(chunk, step).wait_send()
+            far_copy(chunk, step).wait_send()
+            near_copy(chunk, step).wait_send()
+
+    for layer in range(layers):
+        for step in PAGE_ORDER:
+            page_copy(step, layer).wait()
+
+    def place_copy(slot):
+        return pltpu.make_async_copy(pages.at[slot], placed_ref.at[0, slot], place_out.at[slot])
+
+    def place(slot, none):
+        pages[slot] = arrived[sources[slot]]
+        place_copy(slot).start()
+        return none
+
+    def placed(slot, none):
+        place_copy(slot).wait()
+        return none
+
+    lax.fori_loop(0, chips, place, 0)
+    lax.fori_loop(0, chips, placed, 0)
+
+
+def block(
+    tokens, ln_gain, ln_bias, w_qkv, b_qkv, w_out, b_out, kv_cache, prefix_len, kv_pages, page_table
+):
     tp = lax.axis_size("tp")
+    groups = lax.axis_size("grp")
+    page_count, layers, page_len, page_width = kv_pages.shape
+    held = (groups // 2, layers, page_len, page_width // 2)
     rows, width = tokens.shape
     head_count = HEADS // tp
     chunks = rows // ROWS
     bf16 = jnp.bfloat16
     return pl.pallas_call(
-        functools.partial(block_kernel, tp, head_count),
+        functools.partial(block_kernel, tp, groups, head_count),
         name="block",
-        out_shape=jax.ShapeDtypeStruct((rows, width), bf16),
-        in_specs=[ANY, VMEM, VMEM, ANY, VMEM, ANY, VMEM, ANY, SMEM],
-        out_specs=VMEM,
+        out_shape=(
+            jax.ShapeDtypeStruct((rows, width), bf16),
+            jax.ShapeDtypeStruct((1,) + held, bf16),
+            jax.ShapeDtypeStruct((groups, 2, page_count), jnp.int32),
+        ),
+        in_specs=[ANY, VMEM, VMEM, ANY, VMEM, ANY, VMEM, ANY, SMEM, ANY, ANY],
+        out_specs=(VMEM, ANY, ANY),
         scratch_shapes=[
             pltpu.VMEM((tp, rows, width), bf16),
             pltpu.VMEM(w_qkv.shape, bf16),
@@ -475,16 +689,30 @@
             pltpu.VMEM((tp, rows, width), bf16),
             pltpu.VMEM((rows, width), jnp.float32),
             pltpu.SemaphoreType.DMA((4,)),
-            pltpu.SemaphoreType.DMA((chunks, tp)),
-            pltpu.SemaphoreType.DMA((chunks, tp)),
-            pltpu.SemaphoreType.DMA((chunks, tp)),
-            pltpu.SemaphoreType.DMA((chunks, tp)),
+        ]
+        + [pltpu.SemaphoreType.DMA((chunks, tp))] * 8
+        + [pltpu.VMEM(held, bf16)] * 3
+        + [
+            pltpu.VMEM((groups, 2, page_count), jnp.int32),
+            pltpu.SMEM((groups, 2, page_count), jnp.int32),
+            pltpu.SMEM((groups // 2,), jnp.int32),
+            pltpu.SMEM((groups // 2,), jnp.int32),
+            pltpu.SemaphoreType.DMA((page_count,)),
+            pltpu.SemaphoreType.DMA((page_count,)),
+            pltpu.SemaphoreType.DMA((page_count,)),
+            pltpu.SemaphoreType.DMA,
+            pltpu.SemaphoreType.DMA((groups,)),
+            pltpu.SemaphoreType.DMA((groups,)),
+            pltpu.SemaphoreType.DMA((2,)),
+            pltpu.SemaphoreType.DMA((groups // 2, layers)),
+            pltpu.SemaphoreType.DMA((groups // 2, layers)),
+            pltpu.SemaphoreType.DMA((groups // 2,)),
         ],
         cost_estimate=pl.CostEstimate(
             flops=40_000_000_000, bytes_accessed=20_000_000, transcendentals=0
         ),
         compiler_params=pltpu.CompilerParams(
-            collective_id=0, has_side_effects=True, vmem_limit_bytes=56 << 20
+            collective_id=0, has_side_effects=True, vmem_limit_bytes=63 << 20
         ),
     )(
         tokens,
@@ -496,15 +724,31 @@
         b_out[None],
         kv_cache,
         prefix_len,
+        page_table.T,
+        kv_pages,
     )
 
 
 def shards(
     tokens, ln_gain, ln_bias, w_qkv, b_qkv, w_out, b_out, kv_cache, prefix_len, kv_pages, page_table
 ):
-    finish = move_pages(kv_pages, page_table)
-    mixed = block(tokens, ln_gain, ln_bias, w_qkv, b_qkv, w_out, b_out, kv_cache, prefix_len)
-    return (mixed, finish())
+    mixed, placed, tables = block(
+        tokens,
+        ln_gain,
+        ln_bias,
+        w_qkv,
+        b_qkv,
+        w_out,
+        b_out,
+        kv_cache,
+        prefix_len,
+        kv_pages,
+        page_table,
+    )
+    decode_pages = lax.cond(
+        jnp.any(again_in(tables)), lambda moved: move_twice(kv_pages, page_table), lambda moved: moved, placed
+    )
+    return (mixed, decode_pages)
 
 
 def solution(mesh):

time: 147 us -> 121 us (0.82)
  Pallas kernels: 128 us -> 106 us
  starting transfers between devices: 5.85 us -> 0 us
  local copies, waits for them, and re-layouts: 6.11 us -> 10.5 us
  other arithmetic: 3.37 us -> 0.75 us
    pallas_call x4 -> x1, Pallas kernels: 128 us -> 106 us  [block(): pl.pallas_call(functools.partial(block_kernel, tp, groups, head_count), n...]
    all_to_all x1 -> x0, starting transfers between devices: 5.85 us -> none  [exchange(): lax.all_to_all(outgoing, 'grp', split_axis=0, concat_axis=0, tiled=True,...]
    unnamed x6, local copies, waits for them, and re-layouts: 3.62 us -> 8.37 us
  transfers between devices with their start and end apart: 1 -> 0, of which waited for: 0 -> 0; matrix products, arithmetic and copies ran while one was open for 2% -> 0% of each run, Pallas kernels for 72% -> 0%
where the time goes in v2:
time: 121 us; the launch traced here: 119 us
  Pallas kernels  106 us (88%)
  local copies, waits for them, and re-layouts  10.5 us (9%)
  between operations  1.32 us (1%)
    pallas_call x1, Pallas kernels, block(): pl.pallas_call(functools.partial(block_kernel, tp, groups, head_count), n...  106 us
    unnamed x6, local copies, waits for them, and re-layouts  8.37 us

profile of v2, /device:TPU:14, one launch (start us, length us, event | category | flops | bytes accessed | tf_op | source)
XLA Modules:
  0.0 118.6 jit_solution(10408720526324728967)
XLA Ops:
  0.6 1.3 %broadcast_in_dim.47.b_qkv_ref = f32[1,1536]{1,0:T(1,128)} reshape(f32[1536]{0:T(1024)} %param.17) | data formatting | bytes 12288 | tf_op jit(solution)/shard_map/broadcast_in_dim | solution.py:722
  1.9 0.0 copy-start.2
  1.9 106.0 %block.1 = (bf16[1024,512]{1,0:T(8,128)(2,1)}, bf16[1,16,3,128,512]{4,3,2,1,0:T(8,128)(2,1)}, s32[32,2,8]{2,1,0:T(2,128)}) custom-call(bf16[1024,512]{1,0:T(8,128)(2,1)} %tokens_ref.1, f32[1,2048]{1,0:T(1,128)} %bitcast.13, f32[1,2048]{1,0:T(1,128)} %bitcast.14, bf16[2048,1536]{1,0:T(8,128)(2,1)} %w_qkv_ref.1, f32[1,1536]{1,0:T(1,128)} %broadcast_in_dim.47.b_qkv_ref, ...), custom_call_target="tpu_custom_call" | custom-call | flops 40000000000 | bytes 20000000 | tf_op jit(solution)/shard_map/block/pallas_call | solution.py:670
  107.9 0.8 slice_reduce_fusion.1
  108.7 0.1 eq.83
  108.8 0.7 and_reduce_fusion.1
  109.5 0.0 copy-done.2
  110.2 0.0 copy-start
  110.2 1.2 %copy-done = bf16[1024,512]{1,0:T(8,128)(2,1)S(1)} copy-done((bf16[1024,512]{1,0:T(8,128)(2,1)S(1)}, bf16[1024,512]{1,0:T(8,128)(2,1)}, u32[]{:S(2)}) %copy-start) | copy-done | bytes 1048600
  111.4 1.0 copy.21
  112.4 6.2 %copy.22 = bf16[1,16,3,128,512]{4,3,2,1,0:T(8,128)(2,1)} copy(bf16[1,16,3,128,512]{4,3,2,1,0:T(8,128)(2,1)} %get-tuple-element.36) | data formatting | bytes 12582912
  (2 shorter events, 0.0 us)
Async XLA Ops:
  1.9 107.6 %copy-start.2 = (s32[8,2]{0,1:T(2,128)S(1)}, s32[8,2]{0,1:T(2,128)}, u32[]{:S(2)}) copy-start(s32[8,2]{0,1:T(2,128)} %param.23) | copy-start | bytes 196
  110.2 1.2 %copy-start = (bf16[1024,512]{1,0:T(8,128)(2,1)S(1)}, bf16[1024,512]{1,0:T(8,128)(2,1)}, u32[]{:S(2)}) copy-start(bf16[1024,512]{1,0:T(8,128)(2,1)} %get-tuple-element.34) | copy-start | bytes 3145732

commit v3 on v2

--- a/solution.py
+++ b/solution.py
@@ -9,8 +9,9 @@
 
 HEADS = 16
 ROWS = 256
-PAGE_ORDER = (4, 1, 12, 3, 5, 15, 7, 13, 8, 2, 9, 6, 11, 14, 10)
-WIDE = 1024
+PAGE_ORDER = (10, 9, 6, 11, 14, 8, 2, 5, 15, 7, 13, 4, 1, 12, 3)
+WIDE = 512
+TOGETHER = 4
 
 
 NEG = -1e30
@@ -199,6 +200,67 @@
             pltpu.SemaphoreType.DMA((count,)),
         ],
     )(*slots, *valids, *arrived)
+
+
+def finish_kernel(
+    slots, arrived, mixed_ref, placed_ref, out_ref, held, rows, in_sem, out_sem, rows_sem
+):
+    count = arrived.shape[0]
+
+    def into(chip):
+        return pltpu.make_async_copy(arrived.at[chip], held.at[chip], in_sem.at[chip])
+
+    def out_of(chip):
+        return pltpu.make_async_copy(held.at[chip], placed_ref.at[0, slots[chip]], out_sem.at[chip])
+
+    for chip in range(count):
+        into(chip).start()
+    load = pltpu.make_async_copy(mixed_ref, rows, rows_sem.at[0])
+    load.start()
+    for chip in range(count):
+        into(chip).wait()
+        out_of(chip).start()
+    load.wait()
+    save = pltpu.make_async_copy(rows, out_ref, rows_sem.at[1])
+    save.start()
+    for chip in range(count):
+        out_of(chip).wait()
+    save.wait()
+
+
+def place_once(slots, arrived, mixed):
+    count = arrived.shape[0]
+    return pl.pallas_call(
+        finish_kernel,
+        name="place_once",
+        out_shape=(
+            jax.ShapeDtypeStruct((1,) + arrived.shape, arrived.dtype),
+            jax.ShapeDtypeStruct(mixed.shape, mixed.dtype),
+        ),
+        in_specs=[SMEM, ANY, ANY],
+        out_specs=(ANY, ANY),
+        scratch_shapes=[
+            pltpu.VMEM(arrived.shape, arrived.dtype),
+            pltpu.VMEM(mixed.shape, mixed.dtype),
+            pltpu.SemaphoreType.DMA((count,)),
+            pltpu.SemaphoreType.DMA((count,)),
+            pltpu.SemaphoreType.DMA((2,)),
+        ],
+    )(slots, arrived, mixed)
+
+
+def keep_kernel(rows_ref, out_ref):
+    out_ref[...] = rows_ref[...]
+
+
+def keep_rows(rows):
+    return pl.pallas_call(
+        keep_kernel,
+        name="keep_rows",
+        out_shape=jax.ShapeDtypeStruct(rows.shape, rows.dtype),
+        in_specs=[VMEM],
+        out_specs=VMEM,
+    )(rows)
 
 
 def again_in(tables):
@@ -243,23 +305,22 @@
     return place_pages(slots, valids, arrived)
 
 
-def flash(state, queries, keys, values, allowed):
+def score(queries, keys, allowed):
     scores = lax.dot_general(
         queries, keys, (((1,), (1,)), ((), ())), preferred_element_type=jnp.float32
     )
-    if allowed is not None:
-        scores = jnp.where(allowed, scores, NEG)
+    return scores if allowed is None else jnp.where(allowed, scores, NEG)
+
+
+def update(state, scores, values):
     top = jnp.max(scores, axis=1, keepdims=True)
-    if state is None:
-        raised = top
-    else:
-        highest, totals, running = state
-        raised = jnp.maximum(highest, top)
+    raised = top if state is None else jnp.maximum(state[0], top)
     expo = jnp.exp(scores - raised)
     sums = jnp.sum(expo, axis=1, keepdims=True)
     part = jnp.dot(expo.astype(jnp.bfloat16), values, preferred_element_type=jnp.float32)
     if state is None:
         return raised, sums, part
+    highest, totals, running = state
     factor = jnp.exp(highest - raised)
     return raised, totals * factor + sums, running * factor + part
 
@@ -280,8 +341,9 @@
     table_ref,
     pages_ref,
     mixed_ref,
-    placed_ref,
-    tables_ref,
+    arrived,
+    slots,
+    twice_ref,
     whole,
     w_qkv,
     w_out,
@@ -303,11 +365,9 @@
     near_in,
     pages,
     ordered,
-    arrived,
     tables,
     tables_here,
-    slots,
-    sources,
+    powers,
     half_load,
     half_out,
     half_in,
@@ -326,7 +386,7 @@
     partner = group + 1 - 2 * core
     page_count = pages_ref.shape[0]
     layers = pages_ref.shape[1]
-    half_width = placed_ref.shape[-1]
+    half_width = arrived.shape[-1]
     near_columns = pl.ds(pl.multiple_of(core * half_width, half_width), half_width)
     far_columns = pl.ds(pl.multiple_of((1 - core) * half_width, half_width), half_width)
     rows_all, width = tokens_ref.shape
@@ -388,10 +448,15 @@
             device_id_type=MESH,
         )
 
-    def own_copy(chunk, step):
-        rows = rows_of(chunk)
-        sems = tok_out.at[chunk, step], tok_in.at[chunk, step]
+    def own_copy(chunk, step, side):
+        rows = half_of(chunk, side)
+        sems = tok_out.at[chunk, step + side // 2], tok_in.at[chunk, step + side // 2]
         return send(tokens_ref.at[rows], whole.at[me, rows], *sems, step)
+
+    def own_start(chunk):
+        for turn in (0, 2):
+            for step in sides:
+                own_copy(chunk, step, (step + turn) % 4).start()
 
     def relay_copy(chunk, step):
         block = whole.at[lax.rem(me + tp - step, tp), half_of(chunk, step)]
@@ -402,15 +467,14 @@
         sems = far_out.at[chunk, step], far_in.at[chunk, step]
         return send(terms.at[2, rows], got.at[2, rows], *sems, step)
 
-    def near_copy(chunk, step):
-        rows = rows_of(chunk)
-        sems = near_out.at[chunk, step], near_in.at[chunk, step]
+    def near_copy(chunk, step, side):
+        rows = half_of(chunk, side)
+        sems = near_out.at[chunk, step + side // 2], near_in.at[chunk, step + side // 2]
         return send(terms.at[step, rows], got.at[step, rows], *sems, step)
 
     def relay(chunk):
         for step in sides:
-            own_copy(chunk, step).wait_recv()
-        for step in sides:
+            own_copy(chunk, step, step).wait_recv()
             relay_copy(chunk, step).start()
 
     def pass_on(chunk):
@@ -420,8 +484,7 @@
             terms[step, rows, :] = (
                 terms[step, rows, :].astype(jnp.float32) + got[2, rows, :].astype(jnp.float32)
             ).astype(jnp.bfloat16)
-        for step in sides:
-            near_copy(chunk, step).start()
+            near_copy(chunk, step, step).start()
 
     def half_copy(number):
         return pltpu.make_async_remote_copy(
@@ -451,16 +514,19 @@
         table_copy(step).wait()
         return none
 
-    def page_copy(step, layer):
+    piece = pages_ref.shape[2] // 2
+
+    def page_copy(step, part):
+        layer, lines = part // 2, pl.ds(part % 2 * piece, piece)
         down, along = step // side, step % side
         target = (
             lax.rem(chip // side + down, side) * side + lax.rem(lax.rem(chip, side) + along, side)
         )
         return pltpu.make_async_remote_copy(
-            src_ref=ordered.at[target, layer],
-            dst_ref=arrived.at[chip, layer],
-            send_sem=page_out.at[step, layer],
-            recv_sem=page_in.at[step, layer],
+            src_ref=ordered.at[target, layer, lines],
+            dst_ref=arrived.at[chip, layer, lines],
+            send_sem=page_out.at[step, part],
+            recv_sem=page_in.at[step, part],
             device_id={"grp": target * 2 + core},
             device_id_type=MESH,
         )
@@ -474,25 +540,18 @@
             found = jnp.where(request_of(owner, entry) == request, value(entry), found)
         return found
 
-    for step in sides:
-        own_copy(0, step).start()
+    own_start(0)
     for number in range(page_count):
         half_copy(number).start()
     lax.fori_loop(1, groups, start_table, 0)
     relay(0)
-    for step in sides:
-        own_copy(1, step).start()
+    own_start(1)
     for load in loads:
         load.wait()
     lax.fori_loop(1, groups, wait_table, 0)
-    saves = [
-        pltpu.make_async_copy(tables, tables_here, table_save.at[0]),
-        pltpu.make_async_copy(tables, tables_ref, table_save.at[1]),
-    ]
-    for save in saves:
-        save.start()
-    for save in saves:
-        save.wait()
+    save = pltpu.make_async_copy(tables, tables_here, table_save)
+    save.start()
+    save.wait()
     for number in range(page_count):
         half_copy(number).wait()
 
@@ -501,10 +560,11 @@
         return none
 
     lax.fori_loop(0, chips, order_page, 0)
-    arrived[chip] = ordered[chip]
-    for layer in range(layers):
+    stay = pltpu.make_async_copy(ordered.at[chip], arrived.at[chip], place_out)
+    stay.start()
+    for part in range(2 * layers):
         for step in PAGE_ORDER:
-            page_copy(step, layer).start()
+            page_copy(step, part).start()
 
     def slot_from(owner, none):
         slots[owner] = first_of(
@@ -516,14 +576,16 @@
 
     lax.fori_loop(0, chips, slot_from, 0)
 
-    def source_to(slot, none):
-        found = 0
-        for owner in range(chips):
-            found = jnp.where(slots[owner] == slot, owner, found)
-        sources[slot] = found
-        return none
-
-    lax.fori_loop(0, chips, source_to, 0)
+    for request in range(chips):
+        powers[request] = 1 << request
+
+    def repeats(owner, twice):
+        total = 0
+        for entry in range(2 * page_count):
+            total += powers[request_of(owner, entry)]
+        return jnp.where(total == (1 << chips) - 1, twice, 1)
+
+    twice_ref[0] = lax.fori_loop(0, chips, repeats, 0)
 
     length = length_ref[lax.axis_index("grp")]
 
@@ -531,13 +593,15 @@
         rows = rows_of(chunk)
         total = mix[rows, :]
         for step in sides:
-            near_copy(chunk, step).wait_recv()
+            for side in sides:
+                near_copy(chunk, step, side).wait_recv()
             total += got[step, rows, :].astype(jnp.float32)
         mixed_ref[rows, :] = total.astype(jnp.bfloat16)
 
     def visit(chunk, none):
         rows = rows_of(chunk)
         for step in sides:
+            own_copy(chunk, step, 4 - step).wait_recv()
             relay_copy(chunk, step).wait_recv()
         sums = jnp.zeros((ROWS, 1), jnp.float32)
         squares = jnp.zeros((ROWS, 1), jnp.float32)
@@ -558,56 +622,71 @@
             columns = pl.ds(part * part_width, part_width)
             projected = (
                 jnp.dot(normed[...], w_qkv[:, columns], preferred_element_type=jnp.float32)
-                + b_qkv_ref[:, columns]
+                + b_qkv_ref[columns][None, :]
             )
             if part == 0:
                 projected = projected * size ** (-0.5)
             qkv[rows, columns] = projected.astype(jnp.bfloat16)
 
+        @pl.when(chunk + 1 < chunks)
+        def _():
+            relay(chunk + 1)
+
+        for later in range(2, chunks):
+
+            @pl.when(chunk == later - 2)
+            def _():
+                own_start(later)
+
         def head(number, none):
             def lanes(start):
                 return pl.ds(pl.multiple_of(start, size), size)
 
-            @pl.when((number == 0) & (chunk + 1 < chunks))
-            def _():
-                relay(chunk + 1)
-
-            @pl.when((number == 0) & (chunk > 0))
-            def _():
-                pass_on(chunk - 1)
-
-            for later in range(2, chunks):
-
-                @pl.when((chunk == 0) & (number == 2 * (later - 2)))
-                def _():
-                    for step in sides:
-                        own_copy(later, step).start()
-
-            queries = qkv[rows, lanes(number * size)]
-            state = None
+            heads = [number * TOGETHER + other for other in range(TOGETHER)]
+            queries = [qkv[rows, lanes(at * size)] for at in heads]
+
+            def new_block(states, other, allowed):
+                scores = [
+                    score(query, qkv[rows_of(other), lanes(part_width + at * size)], allowed)
+                    for query, at in zip(queries, heads)
+                ]
+                return tuple(
+                    update(state, each, qkv[rows_of(other), lanes(2 * part_width + at * size)])
+                    for state, each, at in zip(states, scores, heads)
+                )
+
+            states = (None,) * TOGETHER
             for block in range(prefix // WIDE):
-                base = block * WIDE
-                keys = cache[pl.ds(base, WIDE), lanes(number * 2 * size)]
-                values = cache[pl.ds(base, WIDE), lanes(number * 2 * size + size)]
-                position = base + lax.broadcasted_iota(jnp.int32, (1, WIDE), 1)
-                state = flash(state, queries, keys, values, position < length)
-
-            def earlier(other, state):
-                keys = qkv[rows_of(other), lanes(part_width + number * size)]
-                values = qkv[rows_of(other), lanes(2 * part_width + number * size)]
-                return flash(state, queries, keys, values, None)
-
-            state = lax.fori_loop(0, chunk, earlier, state)
-            keys = qkv[rows, lanes(part_width + number * size)]
-            values = qkv[rows, lanes(2 * part_width + number * size)]
+                base = pl.ds(block * WIDE, WIDE)
+                position = block * WIDE + lax.broadcasted_iota(jnp.int32, (1, WIDE), 1)
+                scores = [
+                    score(query, cache[base, lanes(at * 2 * size)], position < length)
+                    for query, at in zip(queries, heads)
+                ]
+                states = tuple(
+                    update(state, each, cache[base, lanes(at * 2 * size + size)])
+                    for state, each, at in zip(states, scores, heads)
+                )
+            states = lax.fori_loop(
+                0, chunk, lambda other, states: new_block(states, other, None), states
+            )
             causal = lax.broadcasted_iota(jnp.int32, (ROWS, ROWS), 1) <= lax.broadcasted_iota(
                 jnp.int32, (ROWS, ROWS), 0
             )
-            highest, totals, running = flash(state, queries, keys, values, causal)
-            attended[:, lanes(number * size)] = (running / totals).astype(jnp.bfloat16)
+            states = new_block(states, chunk, causal)
+            for (highest, totals, running), at in zip(states, heads):
+                attended[:, lanes(at * size)] = (running / totals).astype(jnp.bfloat16)
             return none
 
-        lax.fori_loop(0, head_count, head, 0)
+        lax.fori_loop(0, head_count // TOGETHER, head, 0)
+
+        @pl.when(chunk > 0)
+        def _():
+            pass_on(chunk - 1)
+
+        @pl.when(chunk > 1)
+        def _():
+            finish(chunk - 2)
 
         def term(step):
             columns = pl.ds(pl.multiple_of(lax.rem(me + step, tp) * width, width), width)
@@ -618,42 +697,28 @@
             far_copy(chunk, step).start()
         for step in sides:
             terms[step, rows, :] = term(step).astype(jnp.bfloat16)
+            near_copy(chunk, step, 4 - step).start()
         mix[rows, :] = term(0) + whole[me, rows, :].astype(jnp.float32) + b_out_ref[...]
 
-        @pl.when(chunk > 0)
-        def _():
-            finish(chunk - 1)
-
         return none
 
     lax.fori_loop(0, chunks, visit, 0)
+    finish(chunks - 2)
     pass_on(chunks - 1)
     finish(chunks - 1)
     for chunk in range(chunks):
         for step in sides:
-            own_copy(chunk, step).wait_send()
+            for side in sides:
+                own_copy(chunk, step, side).wait_send()
+                near_copy(chunk, step, side).wait_send()
             relay_copy(chunk, step).wait_send()
             far_copy(chunk, step).wait_send()
-            near_copy(chunk, step).wait_send()
-
-    for layer in range(layers):
+
+    for part in range(2 * layers):
         for step in PAGE_ORDER:
-            page_copy(step, layer).wait()
-
-    def place_copy(slot):
-        return pltpu.make_async_copy(pages.at[slot], placed_ref.at[0, slot], place_out.at[slot])
-
-    def place(slot, none):
-        pages[slot] = arrived[sources[slot]]
-        place_copy(slot).start()
-        return none
-
-    def placed(slot, none):
-        place_copy(slot).wait()
-        return none
-
-    lax.fori_loop(0, chips, place, 0)
-    lax.fori_loop(0, chips, placed, 0)
+            page_copy(step, part).wait()
+
+    stay.wait()
 
 
 def block(
@@ -672,11 +737,12 @@
         name="block",
         out_shape=(
             jax.ShapeDtypeStruct((rows, width), bf16),
-            jax.ShapeDtypeStruct((1,) + held, bf16),
-            jax.ShapeDtypeStruct((groups, 2, page_count), jnp.int32),
+            jax.ShapeDtypeStruct(held, bf16),
+            jax.ShapeDtypeStruct((groups // 2,), jnp.int32),
+            jax.ShapeDtypeStruct((1,), jnp.int32),
         ),
         in_specs=[ANY, VMEM, VMEM, ANY, VMEM, ANY, VMEM, ANY, SMEM, ANY, ANY],
-        out_specs=(VMEM, ANY, ANY),
+        out_specs=(VMEM, ANY, SMEM, SMEM),
         scratch_shapes=[
             pltpu.VMEM((tp, rows, width), bf16),
             pltpu.VMEM(w_qkv.shape, bf16),
@@ -690,12 +756,11 @@
             pltpu.VMEM((rows, width), jnp.float32),
             pltpu.SemaphoreType.DMA((4,)),
         ]
-        + [pltpu.SemaphoreType.DMA((chunks, tp))] * 8
-        + [pltpu.VMEM(held, bf16)] * 3
+        + [pltpu.SemaphoreType.DMA((chunks, tp + 2))] * 8
+        + [pltpu.VMEM(held, bf16)] * 2
         + [
             pltpu.VMEM((groups, 2, page_count), jnp.int32),
             pltpu.SMEM((groups, 2, page_count), jnp.int32),
-            pltpu.SMEM((groups // 2,), jnp.int32),
             pltpu.SMEM((groups // 2,), jnp.int32),
             pltpu.SemaphoreType.DMA((page_count,)),
             pltpu.SemaphoreType.DMA((page_count,)),
@@ -703,10 +768,10 @@
             pltpu.SemaphoreType.DMA,
             pltpu.SemaphoreType.DMA((groups,)),
             pltpu.SemaphoreType.DMA((groups,)),
-            pltpu.SemaphoreType.DMA((2,)),
-            pltpu.SemaphoreType.DMA((groups // 2, layers)),
-            pltpu.SemaphoreType.DMA((groups // 2, layers)),
-            pltpu.SemaphoreType.DMA((groups // 2,)),
+            pltpu.SemaphoreType.DMA,
+            pltpu.SemaphoreType.DMA((groups // 2, 2 * layers)),
+            pltpu.SemaphoreType.DMA((groups // 2, 2 * layers)),
+            pltpu.SemaphoreType.DMA,
         ],
         cost_estimate=pl.CostEstimate(
             flops=40_000_000_000, bytes_accessed=20_000_000, transcendentals=0
@@ -719,7 +784,7 @@
         ln_gain[None],
         ln_bias[None],
         w_qkv,
-        b_qkv[None],
+        b_qkv,
         w_out,
         b_out[None],
         kv_cache,
@@ -732,7 +797,7 @@
 def shards(
     tokens, ln_gain, ln_bias, w_qkv, b_qkv, w_out, b_out, kv_cache, prefix_len, kv_pages, page_table
 ):
-    mixed, placed, tables = block(
+    mixed, arrived, slots, twice = block(
         tokens,
         ln_gain,
         ln_bias,
@@ -745,8 +810,13 @@
         kv_pages,
         page_table,
     )
-    decode_pages = lax.cond(
-        jnp.any(again_in(tables)), lambda moved: move_twice(kv_pages, page_table), lambda moved: moved, placed
+    decode_pages, mixed = lax.cond(
+        twice[0] > 0,
+        lambda *once: (move_twice(kv_pages, page_table), keep_rows(once[2])),
+        place_once,
+        slots,
+        arrived,
+        mixed,
     )
     return (mixed, decode_pages)
 

time: 121 us -> 103 us (0.85); the launches traced: 119 us -> 103 us
  local copies, waits for them, and re-layouts: 10.5 us -> 0.97 us
  Pallas kernels: 106 us -> 100 us
    pallas_call x1, Pallas kernels: 106 us -> 94.1 us  [block(): pl.pallas_call(functools.partial(block_kernel, tp, groups, head_count), n...]
    unnamed x6 -> x4, local copies, waits for them, and re-layouts: 8.37 us -> 0.97 us
    pallas_call x0 -> x1, Pallas kernels: none -> 6.04 us  [place_once(): pl.pallas_call(finish_kernel, name='place_once', out_shape=(jax.ShapeDtyp...]
    broadcast_in_dim x1 -> x0, local copies, waits for them, and re-layouts: 1.3 us -> none  [block(): b_qkv[None]]
where the time goes in v3:
time: 103 us
  Pallas kernels  100 us (97%)
  between operations  1.25 us (1%)
    pallas_call x1, Pallas kernels, block(): pl.pallas_call(functools.partial(block_kernel, tp, groups, head_count), n...  94.1 us
    pallas_call x1, Pallas kernels, place_once(): pl.pallas_call(finish_kernel, name='place_once', out_shape=(jax.ShapeDtyp...  6.04 us

profile of v3, /device:TPU:14, one launch (start us, length us, event | category | flops | bytes accessed | tf_op | source)
XLA Modules:
  0.0 102.6 jit_solution(17330976258898581929)
XLA Ops:
  0.6 0.0 copy-start.2
  0.6 94.1 %block.1 = (bf16[1024,512]{1,0:T(8,128)(2,1)}, bf16[16,3,128,512]{3,2,1,0:T(8,128)(2,1)}, s32[16]{0:T(128)S(1)}, s32[1]{0:T(128)}) custom-call(bf16[1024,512]{1,0:T(8,128)(2,1)} %tokens_ref.1, f32[1,2048]{1,0:T(1,128)} %bitcast.14, f32[1,2048]{1,0:T(1,128)} %bitcast.15, bf16[2048,1536]{1,0:T(8,128)(2,1)} %w_qkv_ref.1, f32[1536]{0:T(1024)} %b_qkv_ref.1, ...), custom_call_target="tpu_custom_call" | custom-call | flops 40000000000 | bytes 20000000 | tf_op jit(solution)/shard_map/block/pallas_call | solution.py:735
  95.3 0.0 copy-done.2
  95.3 6.3 %conditional.1 = ((bf16[1,16,3,128,512]{4,3,2,1,0:T(8,128)(2,1)}, bf16[1024,512]{1,0:T(8,128)(2,1)S(1)})) conditional(s32[]{:T(128)} %bitcast.8, (s32[16]{0:T(128)S(1)}, bf16[16,3,128,512]{3,2,1,0:T(8,128)(2,1)}, bf16[1024,512]{1,0:T(8,128)(2,1)}) %tuple.15, (s32[8,2]{0,1:T(2,128)S(1)}, bf16[8,3,128,1024]{3,2,1,0:T(8,128)(2,1)}, ...), branch_computations={%region_0.0_spmd, %region_1.13_spmd} | conditional | flops 16826 | bytes 41963524 | solution.py:813
  95.4 6.0 %place_once.1 = (bf16[1,16,3,128,512]{4,3,2,1,0:T(8,128)(2,1)}, bf16[1024,512]{1,0:T(8,128)(2,1)S(1)}) custom-call(s32[16]{0:T(128)S(1)} %get-tuple-element.12.slots, bf16[16,3,128,512]{3,2,1,0:T(8,128)(2,1)} %get-tuple-element.13.arrived, bf16[1024,512]{1,0:T(8,128)(2,1)} %get-tuple-element.14.mixed_ref), custom_call_target="tpu_custom_call" | custom-call | tf_op jit(solution)/shard_map/cond/branch_0_fun/place_once/pallas_call | solution.py:233
  101.6 0.0 copy-start.3
  101.6 1.0 copy-done.3
Async XLA Ops:
  0.6 94.7 %copy-start.2 = (s32[8,2]{0,1:T(2,128)S(1)}, s32[8,2]{0,1:T(2,128)}, u32[]{:S(2)}) copy-start(s32[8,2]{0,1:T(2,128)} %param.23) | copy-start | bytes 196
  101.6 1.0 copy-start.3

commit v4 on v3

--- a/solution.py
+++ b/solution.py
@@ -9,6 +9,7 @@
 
 HEADS = 16
 ROWS = 256
+PARTS = 6
 PAGE_ORDER = (10, 9, 6, 11, 14, 8, 2, 5, 15, 7, 13, 4, 1, 12, 3)
 WIDE = 512
 TOGETHER = 4
@@ -238,7 +239,7 @@
             jax.ShapeDtypeStruct(mixed.shape, mixed.dtype),
         ),
         in_specs=[SMEM, ANY, ANY],
-        out_specs=(ANY, ANY),
+        out_specs=(ANY, pl.BlockSpec(memory_space=pltpu.HBM)),
         scratch_shapes=[
             pltpu.VMEM(arrived.shape, arrived.dtype),
             pltpu.VMEM(mixed.shape, mixed.dtype),
@@ -250,7 +251,7 @@
 
 
 def keep_kernel(rows_ref, out_ref):
-    out_ref[...] = rows_ref[...]
+    pltpu.sync_copy(rows_ref, out_ref)
 
 
 def keep_rows(rows):
@@ -259,7 +260,7 @@
         name="keep_rows",
         out_shape=jax.ShapeDtypeStruct(rows.shape, rows.dtype),
         in_specs=[VMEM],
-        out_specs=VMEM,
+        out_specs=pl.BlockSpec(memory_space=pltpu.HBM),
     )(rows)
 
 
@@ -363,11 +364,11 @@
     far_in,
     near_out,
     near_in,
-    pages,
     ordered,
     tables,
     tables_here,
     powers,
+    picks,
     half_load,
     half_out,
     half_in,
@@ -378,6 +379,7 @@
     page_out,
     page_in,
     place_out,
+    *pages,
 ):
     me = lax.axis_index("tp")
     group = lax.axis_index("grp")
@@ -404,15 +406,23 @@
         pltpu.make_async_copy(cache_ref, cache, load_sem.at[2]),
         pltpu.make_async_copy(w_out_ref, w_out, load_sem.at[3]),
     ]
-    loads += [
-        pltpu.make_async_copy(
-            pages_ref.at[number, :, :, near_columns],
-            pages.at[core * page_count + number],
-            half_load.at[number],
-        )
-        for number in range(page_count)
-    ]
-    loads.append(pltpu.make_async_copy(table_ref, tables.at[group], table_load))
+    parts = len(pages)
+    piece = pages_ref.shape[2] * layers // parts
+    ours = pl.ds(pl.multiple_of(core * page_count, page_count), page_count)
+
+    def place_of(part):
+        layer, line = divmod(part * piece, pages_ref.shape[2])
+        return layer, pl.ds(line, piece)
+
+    def piece_load(part):
+        return pltpu.make_async_copy(
+            pages_ref.at[:, *place_of(part), near_columns], pages[part].at[ours], half_load.at[part]
+        )
+
+    table_own = pltpu.make_async_copy(table_ref, tables.at[group], table_load)
+    table_own.start()
+    for part in range(parts):
+        piece_load(part).start()
     for load in loads:
         load.start()
 
@@ -486,12 +496,12 @@
             ).astype(jnp.bfloat16)
             near_copy(chunk, step, step).start()
 
-    def half_copy(number):
+    def half_copy(part):
         return pltpu.make_async_remote_copy(
-            src_ref=pages_ref.at[number, :, :, far_columns],
-            dst_ref=pages.at[core * page_count + number],
-            send_sem=half_out.at[number],
-            recv_sem=half_in.at[number],
+            src_ref=pages_ref.at[:, *place_of(part), far_columns],
+            dst_ref=pages[part].at[ours],
+            send_sem=half_out.at[part],
+            recv_sem=half_in.at[part],
             device_id={"grp": partner},
             device_id_type=MESH,
         )
@@ -514,17 +524,14 @@
         table_copy(step).wait()
         return none
 
-    piece = pages_ref.shape[2] // 2
-
     def page_copy(step, part):
-        layer, lines = part // 2, pl.ds(part % 2 * piece, piece)
         down, along = step // side, step % side
         target = (
             lax.rem(chip // side + down, side) * side + lax.rem(lax.rem(chip, side) + along, side)
         )
         return pltpu.make_async_remote_copy(
-            src_ref=ordered.at[target, layer, lines],
-            dst_ref=arrived.at[chip, layer, lines],
+            src_ref=ordered.at[target, *place_of(part)],
+            dst_ref=arrived.at[chip, *place_of(part)],
             send_sem=page_out.at[step, part],
             recv_sem=page_in.at[step, part],
             device_id={"grp": target * 2 + core},
@@ -541,30 +548,45 @@
         return found
 
     own_start(0)
-    for number in range(page_count):
-        half_copy(number).start()
+    for part in range(parts):
+        half_copy(part).start()
     lax.fori_loop(1, groups, start_table, 0)
     relay(0)
     own_start(1)
-    for load in loads:
-        load.wait()
+    own_start(2)
+    table_own.wait()
     lax.fori_loop(1, groups, wait_table, 0)
     save = pltpu.make_async_copy(tables, tables_here, table_save)
     save.start()
     save.wait()
-    for number in range(page_count):
-        half_copy(number).wait()
-
-    def order_page(request, none):
-        ordered[request] = pages[first_of(chip, request, lambda entry: entry)]
+
+    def pick(request, none):
+        picks[request] = first_of(chip, request, lambda entry: entry)
         return none
 
-    lax.fori_loop(0, chips, order_page, 0)
+    lax.fori_loop(0, chips, pick, 0)
+
+    def send_pieces(part):
+        for step in PAGE_ORDER:
+            page_copy(step, part).start()
+
+    for part in range(parts):
+        piece_load(part).wait()
+        half_copy(part).wait_recv()
+        layer, lines = place_of(part)
+
+        def order_piece(request, none):
+            ordered[request, layer, lines] = pages[part][picks[request]]
+            return none
+
+        lax.fori_loop(0, chips, order_piece, 0)
+        if part:
+            send_pieces(part - 1)
+    send_pieces(parts - 1)
     stay = pltpu.make_async_copy(ordered.at[chip], arrived.at[chip], place_out)
     stay.start()
-    for part in range(2 * layers):
-        for step in PAGE_ORDER:
-            page_copy(step, part).start()
+    for load in loads:
+        load.wait()
 
     def slot_from(owner, none):
         slots[owner] = first_of(
@@ -599,6 +621,16 @@
         mixed_ref[rows, :] = total.astype(jnp.bfloat16)
 
     def visit(chunk, none):
+        @pl.when(chunk + 1 < chunks)
+        def _():
+            relay(chunk + 1)
+
+        for later in range(3, chunks):
+
+            @pl.when(chunk == later - 3)
+            def _():
+                own_start(later)
+
         rows = rows_of(chunk)
         for step in sides:
             own_copy(chunk, step, 4 - step).wait_recv()
@@ -628,16 +660,6 @@
                 projected = projected * size ** (-0.5)
             qkv[rows, columns] = projected.astype(jnp.bfloat16)
 
-        @pl.when(chunk + 1 < chunks)
-        def _():
-            relay(chunk + 1)
-
-        for later in range(2, chunks):
-
-            @pl.when(chunk == later - 2)
-            def _():
-                own_start(later)
-
         def head(number, none):
             def lanes(start):
                 return pl.ds(pl.multiple_of(start, size), size)
@@ -714,7 +736,8 @@
             relay_copy(chunk, step).wait_send()
             far_copy(chunk, step).wait_send()
 
-    for part in range(2 * layers):
+    for part in range(parts):
+        half_copy(part).wait_send()
         for step in PAGE_ORDER:
             page_copy(step, part).wait()
 
@@ -757,22 +780,24 @@
             pltpu.SemaphoreType.DMA((4,)),
         ]
         + [pltpu.SemaphoreType.DMA((chunks, tp + 2))] * 8
-        + [pltpu.VMEM(held, bf16)] * 2
         + [
+            pltpu.VMEM(held, bf16),
             pltpu.VMEM((groups, 2, page_count), jnp.int32),
             pltpu.SMEM((groups, 2, page_count), jnp.int32),
             pltpu.SMEM((groups // 2,), jnp.int32),
-            pltpu.SemaphoreType.DMA((page_count,)),
-            pltpu.SemaphoreType.DMA((page_count,)),
-            pltpu.SemaphoreType.DMA((page_count,)),
+            pltpu.SMEM((groups // 2,), jnp.int32),
+            pltpu.SemaphoreType.DMA((PARTS,)),
+            pltpu.SemaphoreType.DMA((PARTS,)),
+            pltpu.SemaphoreType.DMA((PARTS,)),
             pltpu.SemaphoreType.DMA,
             pltpu.SemaphoreType.DMA((groups,)),
             pltpu.SemaphoreType.DMA((groups,)),
             pltpu.SemaphoreType.DMA,
-            pltpu.SemaphoreType.DMA((groups // 2, 2 * layers)),
-            pltpu.SemaphoreType.DMA((groups // 2, 2 * layers)),
+            pltpu.SemaphoreType.DMA((groups // 2, PARTS)),
+            pltpu.SemaphoreType.DMA((groups // 2, PARTS)),
             pltpu.SemaphoreType.DMA,
-        ],
+        ]
+        + [pltpu.VMEM((held[0], layers * page_len // PARTS, held[3]), bf16)] * PARTS,
         cost_estimate=pl.CostEstimate(
             flops=40_000_000_000, bytes_accessed=20_000_000, transcendentals=0
         ),

time: 103 us -> 103 us (level)
  no operation moved by 1% of the time
where the time goes in v4:
time: 103 us; the launch traced here: 102 us
  Pallas kernels  100 us (97%)
  between operations  1.25 us (1%)
    pallas_call x1, Pallas kernels, block(): pl.pallas_call(functools.partial(block_kernel, tp, groups, head_count), n...  93.9 us
    pallas_call x1, Pallas kernels, place_once(): pl.pallas_call(finish_kernel, name='place_once', out_shape=(jax.ShapeDtyp...  6.04 us

profile of v4, /device:TPU:14, one launch (start us, length us, event | category | flops | bytes accessed | tf_op | source)
XLA Modules:
  0.0 102.4 jit_solution(13326337416646424322)
XLA Ops:
  0.6 0.0 copy-start.2
  0.6 93.9 %block.1 = (bf16[1024,512]{1,0:T(8,128)(2,1)}, bf16[16,3,128,512]{3,2,1,0:T(8,128)(2,1)}, s32[16]{0:T(128)S(1)}, s32[1]{0:T(128)}) custom-call(bf16[1024,512]{1,0:T(8,128)(2,1)} %tokens_ref.1, f32[1,2048]{1,0:T(1,128)} %bitcast.14, f32[1,2048]{1,0:T(1,128)} %bitcast.15, bf16[2048,1536]{1,0:T(8,128)(2,1)} %w_qkv_ref.1, f32[1536]{0:T(1024)} %b_qkv_ref.1, ...), custom_call_target="tpu_custom_call" | custom-call | flops 40000000000 | bytes 20000000 | tf_op jit(solution)/shard_map/block/pallas_call | solution.py:758
  95.2 0.0 copy-done.2
  95.2 6.3 %conditional.1 = ((bf16[1,16,3,128,512]{4,3,2,1,0:T(8,128)(2,1)}, bf16[1024,512]{1,0:T(8,128)(2,1)S(1)})) conditional(s32[]{:T(128)} %bitcast.8, (s32[16]{0:T(128)S(1)}, bf16[16,3,128,512]{3,2,1,0:T(8,128)(2,1)}, bf16[1024,512]{1,0:T(8,128)(2,1)}) %tuple.15, (s32[8,2]{0,1:T(2,128)S(1)}, bf16[8,3,128,1024]{3,2,1,0:T(8,128)(2,1)}, ...), branch_computations={%region_0.0_spmd, %region_1.13_spmd} | conditional | flops 16826 | bytes 41963524 | solution.py:838
  95.2 6.0 %place_once.1 = (bf16[1,16,3,128,512]{4,3,2,1,0:T(8,128)(2,1)}, bf16[1024,512]{1,0:T(8,128)(2,1)S(1)}) custom-call(s32[16]{0:T(128)S(1)} %get-tuple-element.12.slots, bf16[16,3,128,512]{3,2,1,0:T(8,128)(2,1)} %get-tuple-element.13.arrived, bf16[1024,512]{1,0:T(8,128)(2,1)} %get-tuple-element.14.mixed_ref), custom_call_target="tpu_custom_call" | custom-call | tf_op jit(solution)/shard_map/cond/branch_0_fun/place_once/pallas_call | solution.py:234
  101.5 0.0 copy-start.3
  101.5 1.0 copy-done.3
Async XLA Ops:
  0.6 94.5 %copy-start.2 = (s32[8,2]{0,1:T(2,128)S(1)}, s32[8,2]{0,1:T(2,128)}, u32[]{:S(2)}) copy-start(s32[8,2]{0,1:T(2,128)} %param.23) | copy-start | bytes 196
  101.5 1.0 copy-start.3

commit v5 on v4

--- a/solution.py
+++ b/solution.py
@@ -208,24 +208,30 @@
 ):
     count = arrived.shape[0]
 
-    def into(chip):
-        return pltpu.make_async_copy(arrived.at[chip], held.at[chip], in_sem.at[chip])
-
-    def out_of(chip):
-        return pltpu.make_async_copy(held.at[chip], placed_ref.at[0, slots[chip]], out_sem.at[chip])
-
-    for chip in range(count):
-        into(chip).start()
+    pieces = [(chip, layer) for chip in range(count) for layer in range(arrived.shape[1])]
+
+    def into(chip, layer):
+        return pltpu.make_async_copy(
+            arrived.at[chip, layer], held.at[chip, layer], in_sem.at[chip, layer]
+        )
+
+    def out_of(chip, layer):
+        return pltpu.make_async_copy(
+            held.at[chip, layer], placed_ref.at[0, slots[chip], layer], out_sem.at[chip, layer]
+        )
+
+    for each in pieces:
+        into(*each).start()
     load = pltpu.make_async_copy(mixed_ref, rows, rows_sem.at[0])
     load.start()
-    for chip in range(count):
-        into(chip).wait()
-        out_of(chip).start()
+    for each in pieces:
+        into(*each).wait()
+        out_of(*each).start()
     load.wait()
     save = pltpu.make_async_copy(rows, out_ref, rows_sem.at[1])
     save.start()
-    for chip in range(count):
-        out_of(chip).wait()
+    for each in pieces:
+        out_of(*each).wait()
     save.wait()
 
 
@@ -243,10 +249,11 @@
         scratch_shapes=[
             pltpu.VMEM(arrived.shape, arrived.dtype),
             pltpu.VMEM(mixed.shape, mixed.dtype),
-            pltpu.SemaphoreType.DMA((count,)),
-            pltpu.SemaphoreType.DMA((count,)),
+            pltpu.SemaphoreType.DMA(arrived.shape[:2]),
+            pltpu.SemaphoreType.DMA(arrived.shape[:2]),
             pltpu.SemaphoreType.DMA((2,)),
         ],
+        compiler_params=pltpu.CompilerParams(vmem_limit_bytes=63 << 20),
     )(slots, arrived, mixed)
 
 
@@ -261,6 +268,7 @@
         out_shape=jax.ShapeDtypeStruct(rows.shape, rows.dtype),
         in_specs=[VMEM],
         out_specs=pl.BlockSpec(memory_space=pltpu.HBM),
+        compiler_params=pltpu.CompilerParams(vmem_limit_bytes=63 << 20),
     )(rows)
 
 

time: 103 us -> 103 us (level)
  Pallas kernels: 100 us -> 102 us
    pallas_call x1, Pallas kernels: 6.04 us -> 7.7 us  [place_once(): pl.pallas_call(finish_kernel, name='place_once', out_shape=(jax.ShapeDtyp...]
where the time goes in v5:
time: 103 us
  Pallas kernels  102 us (99%)
  between operations  1.41 us (1%)
    pallas_call x1, Pallas kernels, block(): pl.pallas_call(functools.partial(block_kernel, tp, groups, head_count), n...  93.9 us
    pallas_call x1, Pallas kernels, place_once(): pl.pallas_call(finish_kernel, name='place_once', out_shape=(jax.ShapeDtyp...  7.7 us

profile of v5, /device:TPU:14, one launch (start us, length us, event | category | flops | bytes accessed | tf_op | source)
XLA Modules:
  0.0 103.3 jit_solution(6998569553206437572)
XLA Ops:
  0.6 0.0 copy-start.1
  0.6 93.9 %block.1 = (bf16[1024,512]{1,0:T(8,128)(2,1)}, bf16[16,3,128,512]{3,2,1,0:T(8,128)(2,1)}, s32[16]{0:T(128)S(1)}, s32[1]{0:T(128)}) custom-call(bf16[1024,512]{1,0:T(8,128)(2,1)} %tokens_ref.1, f32[1,2048]{1,0:T(1,128)} %bitcast.14, f32[1,2048]{1,0:T(1,128)} %bitcast.15, bf16[2048,1536]{1,0:T(8,128)(2,1)} %w_qkv_ref.1, f32[1536]{0:T(1024)} %b_qkv_ref.1, ...), custom_call_target="tpu_custom_call" | custom-call | flops 40000000000 | bytes 20000000 | tf_op jit(solution)/shard_map/block/pallas_call | solution.py:766
  95.2 0.0 copy-done.1
  95.2 7.9 %conditional.1 = ((bf16[1,16,3,128,512]{4,3,2,1,0:T(8,128)(2,1)}, bf16[1024,512]{1,0:T(8,128)(2,1)})) conditional(s32[]{:T(128)} %bitcast.8, (s32[16]{0:T(128)S(1)}, bf16[16,3,128,512]{3,2,1,0:T(8,128)(2,1)}, bf16[1024,512]{1,0:T(8,128)(2,1)}) %tuple.15, (s32[8,2]{0,1:T(2,128)S(1)}, bf16[8,3,128,1024]{3,2,1,0:T(8,128)(2,1)}, ...), branch_computations={%region_0.0_spmd, %region_1.13_spmd} | conditional | flops 16826 | bytes 37769192 | solution.py:846
  95.2 7.7 %place_once.1 = (bf16[1,16,3,128,512]{4,3,2,1,0:T(8,128)(2,1)}, bf16[1024,512]{1,0:T(8,128)(2,1)}) custom-call(s32[16]{0:T(128)S(1)} %get-tuple-element.12.slots, bf16[16,3,128,512]{3,2,1,0:T(8,128)(2,1)} %get-tuple-element.13.arrived, bf16[1024,512]{1,0:T(8,128)(2,1)} %get-tuple-element.14.mixed_ref), custom_call_target="tpu_custom_call" | custom-call | tf_op jit(solution)/shard_map/cond/branch_0_fun/place_once/pallas_call | solution.py:240
Async XLA Ops:
  0.6 94.5 %copy-start.1 = (s32[8,2]{0,1:T(2,128)S(1)}, s32[8,2]{0,1:T(2,128)}, u32[]{:S(2)}) copy-start(s32[8,2]{0,1:T(2,128)} %param.23) | copy-start | bytes 196
